TPU v7x, 128 devices: a whole 4x4x4 slice. The times are simulated.
128 devices in a mesh: dom: 32 (over z, x, core), feat: 4 (over y).
Axes of the slice: x: 4, y: 4, z: 4, core: 2. Of those that a mesh axis runs over, the one named last changes fastest.
Arguments:
- feats: bfloat16 [65536, 768], P('dom', 'feat'), may hold values from -6 to 6
- tile_vals: bfloat16 [6144, 128, 128], P('dom'), may hold values from 0 to 1
- tile_dst: int32 [6144], P('dom'), may hold values from 0 to 15
- tile_src: int32 [6144], P('dom'), may hold values from 0 to 79
- tile_count: int32 [32], P('dom'), may hold values from 96 to 192, as said below
- send_blocks: int32 [32, 8, 8], P('dom'), may hold values from 0 to 15
- send_count: int32 [32, 8], P('dom'), may hold values from 1 to 8, as said below
- w_self: bfloat16 [3, 768, 768], replicated, may hold values from -0.21875 to 0.21875
- w_nbr: bfloat16 [3, 768, 768], replicated, may hold values from -0.21875 to 0.21875
- bias: float32 [3, 768], replicated, may hold values from -3 to 3
Outputs:
- hidden: bfloat16 [65536, 768], P('dom', 'feat')
Inputs may be any that keep to these rules, and one draw needn't show every extreme that they name: `tile_count`: some partition has exactly 192 live tiles. `send_count`: some partition sends exactly 8 blocks to some peer.
All inputs are finite; a program needn't handle non-finite values.
Results may differ from a plain program's by a relative error of at most 0.0085.
Values may be sent and summed in bfloat16 or wider, within the bound.
A program may use at most 128 MiB of HBM per device.

v0:
```python
import jax
import jax.numpy as jnp
from jax import lax
from jax.sharding import PartitionSpec as P

LAYERS = 3
BLK = 128
PEERS = 8
SLOTS = 8


def from_behind(block, axis, distance):
    devices = range(lax.axis_size(axis))
    route = [((i - distance) % len(devices), i) for i in devices]
    return lax.ppermute(block, axis, route)


def per_device(
    feats, tile_vals, tile_dst, tile_src, tile_count, send_blocks, send_count, w_self, w_nbr, bias
):
    node_rows, cols = feats.shape
    blk_dev = node_rows // BLK
    tiles_here = tile_vals.shape[0]
    column_start = lax.axis_index("feat") * cols
    offsets = [(d // 2 + 1) * (1 if d % 2 == 0 else -1) for d in range(PEERS)]
    live = (jnp.arange(tiles_here, dtype=jnp.int32) < tile_count[0]).astype(jnp.bfloat16)
    masked = tile_vals * live[:, None, None]
    onehot = (tile_dst[None, :] == jnp.arange(blk_dev, dtype=jnp.int32)[:, None]).astype(
        jnp.float32
    )
    row_sums = jnp.sum(masked.astype(jnp.float32), axis=2)
    degree = 1.0 + jnp.dot(onehot, row_sums, preferred_element_type=jnp.float32)
    slot_ids = jnp.arange(SLOTS, dtype=jnp.int32)
    hidden = feats
    for layer in range(LAYERS):
        blocks_here = hidden.reshape(blk_dev, BLK, cols)
        outgoing = []
        for d in range(PEERS):
            filled = (slot_ids < send_count[0, d]).astype(jnp.bfloat16)
            outgoing.append(blocks_here[send_blocks[0, d]] * filled[:, None, None])
        incoming = [None] * PEERS
        for d in range(PEERS):
            incoming[d] = from_behind(outgoing[d], "dom", offsets[d])
        received = jnp.stack(incoming).reshape(PEERS * SLOTS, BLK, cols)
        source_list = jnp.concatenate([blocks_here, received], axis=0)
        picked = source_list[tile_src]
        contrib = jnp.einsum("tij,tjf->tif", masked, picked, preferred_element_type=jnp.float32)
        summed = jnp.einsum("bt,tif->bif", onehot, contrib, preferred_element_type=jnp.float32)
        agg_blocks = (summed / degree[:, :, None]).astype(jnp.bfloat16)
        agg = agg_blocks.reshape(node_rows, cols)
        last_layer = layer == LAYERS - 1
        bias_here = lax.dynamic_slice_in_dim(bias[layer], column_start, cols, 0)
        self_cols = lax.dynamic_slice_in_dim(w_self[layer], column_start, cols, 1)
        nbr_cols = lax.dynamic_slice_in_dim(w_nbr[layer], column_start, cols, 1)
        total = jnp.dot(
            lax.all_gather(hidden, "feat", axis=1, tiled=True),
            self_cols,
            preferred_element_type=jnp.float32,
        )
        pre = total + jnp.dot(
            lax.all_gather(agg, "feat", axis=1, tiled=True),
            nbr_cols,
            preferred_element_type=jnp.float32,
        )
        pre = pre + bias_here[None, :]
        if not last_layer:
            pre = jax.nn.relu(pre)
        hidden = pre.astype(jnp.bfloat16)
    return hidden


def solution(mesh):
    in_specs = (
        P("dom", "feat"),
        P("dom", None, None),
        P("dom"),
        P("dom"),
        P("dom"),
        P("dom", None, None),
        P("dom", None),
        P(),
        P(),
        P(),
    )
    out_specs = P("dom", "feat")
    return jax.shard_map(
        per_device, mesh=mesh, in_specs=in_specs, out_specs=out_specs, check_vma=False
    )
```

profile of v0, /device:TPU:0, one launch (start us, length us, event | category | flops | bytes accessed | tf_op | source)
XLA Modules:
  0.0 449.2 jit_solution(2568618294756694996)
XLA Ops:
  9.6 1.6 fusion.68
  15.5 5.8 %collective-permute-start.1 = (bf16[8,128,192]{1,2,0:T(8,128)(2,1)}, bf16[8,128,192]{1,2,0:T(8,128)(2,1)S(1)}, u32[]{:S(2)}, u32[]{:S(2)}) collective-permute-start(bf16[8,128,192]{1,2,0:T(8,128)(2,1)} %broadcast_multiply_fusion.20), channel_id=1, source_target_pairs={{4,0},{8,4},{12,8},{16,12},{20,16},{24,20},{28,24},{32,28},{36,32}... | collective-permute-start | bytes 1179656 | tf_op jit(solution)/shard_map/ppermute | solution.py:15
  25.7 5.3 %collective-permute-start.3 = (bf16[8,128,192]{1,2,0:T(8,128)(2,1)}, bf16[8,128,192]{1,2,0:T(8,128)(2,1)S(1)}, u32[]{:S(2)}, u32[]{:S(2)}) collective-permute-start(bf16[8,128,192]{1,2,0:T(8,128)(2,1)} %broadcast_multiply_fusion.14), channel_id=1, source_target_pairs={{8,0},{12,4},{16,8},{20,12},{24,16},{28,20},{32,24},{36,28},{40,32... | collective-permute-start | bytes 1179656 | tf_op jit(solution)/shard_map/ppermute | solution.py:15
  38.2 6.4 %convert_reduce_fusion = bf16[192,128]{1,0:T(8,128)(2,1)S(1)} fusion(bf16[192,128,128]{2,1,0:T(8,128)(2,1)} %param.11, bf16[192]{0:T(256)(128)(2,1)S(1)} %compare_convert_fusion.8), kind=kLoop, calls=%fused_computation.33 | loop fusion | flops 15704064 | bytes 6340992 | tf_op jit(solution)/shard_map/reduce_sum | solution.py:31
  44.8 5.4 %collective-permute-start.5 = (bf16[8,128,192]{1,2,0:T(8,128)(2,1)S(1)}, bf16[8,128,192]{1,2,0:T(8,128)(2,1)S(1)}, u32[]{:S(2)}, u32[]{:S(2)}) collective-permute-start(bf16[8,128,192]{1,2,0:T(8,128)(2,1)S(1)} %broadcast_multiply_fusion.8), channel_id=1, source_target_pairs={{12,0},{16,4},{20,8},{24,12},{28,16},{32,20},{36,24},{40,28},{44,3... | collective-permute-start | bytes 1179656 | tf_op jit(solution)/shard_map/ppermute | solution.py:15
  50.4 5.7 %collective-permute-start.7 = (bf16[8,128,192]{1,2,0:T(8,128)(2,1)S(1)}, bf16[8,128,192]{1,2,0:T(8,128)(2,1)S(1)}, u32[]{:S(2)}, u32[]{:S(2)}) collective-permute-start(bf16[8,128,192]{1,2,0:T(8,128)(2,1)S(1)} %broadcast_multiply_fusion.2), channel_id=1, source_target_pairs={{16,0},{20,4},{24,8},{28,12},{32,16},{36,20},{40,24},{44,28},{48,3... | collective-permute-start | bytes 1179656 | tf_op jit(solution)/shard_map/ppermute | solution.py:15
  57.3 2.4 collective-permute-done.5
  59.8 6.0 %collective-permute-done.6 = bf16[8,128,192]{1,2,0:T(8,128)(2,1)S(1)} collective-permute-done((bf16[8,128,192]{1,2,0:T(8,128)(2,1)S(1)}, bf16[8,128,192]{1,2,0:T(8,128)(2,1)S(1)}, u32[]{:S(2)}, u32[]{:S(2)}) %collective-permute-start.6) | collective-permute-done | bytes 393248 | tf_op jit(solution)/shard_map/ppermute | solution.py:15
  65.8 2.3 collective-permute-done.7
  68.2 2.3 pad_maximum_fusion
  70.6 12.0 %gather_fusion.8 = bf16[192,128,192]{1,2,0:T(8,128)(2,1)} fusion(bf16[80,128,192]{1,2,0:T(8,128)(2,1)} %pad_maximum_fusion, s32[1024]{0:T(1024)S(1)} %pad_clamp_fusion), kind=kCustom, calls=%fused_computation.8 | custom fusion | bytes 18875136 | tf_op jit(solution)/shard_map/gather | solution.py:46
  82.6 15.7 %fusion.10 = bf16[192,128,192]{1,2,0:T(8,128)(2,1)} fusion(bf16[192,128,192]{1,2,0:T(8,128)(2,1)} %gather_fusion.8, bf16[192,128,128]{2,1,0:T(8,128)(2,1)} %param.11, bf16[192]{0:T(256)(128)(2,1)S(1)} %compare_convert_fusion.8), kind=kOutput, calls=%fused_computation.38 | convolution fusion | flops 1211105280 | bytes 25166208 | tf_op jit(solution)/shard_map/tij,tjf->tif/dot_general | solution.py:47
  98.3 8.9 %divide_convert_fusion.2 = bf16[16,128,192]{1,0,2:T(8,128)(2,1)S(1)} fusion(bf16[192,128,192]{1,2,0:T(8,128)(2,1)} %fusion.10, f32[16,128]{1,0:T(8,128)S(1)} %convolution_add_fusion.3, s32[192]{0:T(256)} %param.12), kind=kOutput, calls=%fused_computation.60 | convolution fusion | flops 151784448 | bytes 10232576 | tf_op jit(solution)/shard_map/bt,tif->bif/dot_general | solution.py:48
  108.9 1.4 fusion.67
  110.4 1.9 fusion.66
  112.3 1.4 copy-done.1
  113.6 1.7 fusion.65
  115.3 3.0 convolution_bitcast_fusion
  118.3 35.4 %all-gather.9.cloned.1.call-done = bf16[2048,768]{0,1:T(8,128)(2,1)} async-done(((bf16[2048,192]{0,1:T(8,128)(2,1)}), bf16[2048,768]{0,1:T(8,128)(2,1)}) %all-gather.9.cloned.1.call-update) | async-done | bytes 3145744 | tf_op jit(solution)/shard_map/all_gather | solution.py:61
  153.7 3.7 fusion.21
  157.5 1.3 copy_bitcast_fusion.4
  158.8 1.5 gather_fusion.9
  166.9 5.1 %collective-permute-start.9 = (bf16[8,128,192]{1,2,0:T(8,128)(2,1)S(1)}, bf16[8,128,192]{1,2,0:T(8,128)(2,1)S(1)}, u32[]{:S(2)}, u32[]{:S(2)}) collective-permute-start(bf16[8,128,192]{1,2,0:T(8,128)(2,1)S(1)} %broadcast_multiply_fusion.19), channel_id=1, source_target_pairs={{4,0},{8,4},{12,8},{16,12},{20,16},{24,20},{28,24},{32,28},{36,32}... | collective-permute-start | bytes 1179656 | tf_op jit(solution)/shard_map/ppermute | solution.py:15
  173.7 5.4 %collective-permute-start.11 = (bf16[8,128,192]{1,2,0:T(8,128)(2,1)S(1)}, bf16[8,128,192]{1,2,0:T(8,128)(2,1)S(1)}, u32[]{:S(2)}, u32[]{:S(2)}) collective-permute-start(bf16[8,128,192]{1,2,0:T(8,128)(2,1)S(1)} %broadcast_multiply_fusion.13), channel_id=1, source_target_pairs={{8,0},{12,4},{16,8},{20,12},{24,16},{28,20},{32,24},{36,28},{40,32... | collective-permute-start | bytes 1179656 | tf_op jit(solution)/shard_map/ppermute | solution.py:15
  180.8 5.4 %collective-permute-start.13 = (bf16[8,128,192]{1,2,0:T(8,128)(2,1)S(1)}, bf16[8,128,192]{1,2,0:T(8,128)(2,1)S(1)}, u32[]{:S(2)}, u32[]{:S(2)}) collective-permute-start(bf16[8,128,192]{1,2,0:T(8,128)(2,1)S(1)} %broadcast_multiply_fusion.7), channel_id=1, source_target_pairs={{12,0},{16,4},{20,8},{24,12},{28,16},{32,20},{36,24},{40,28},{44,3... | collective-permute-start | bytes 1179656 | tf_op jit(solution)/shard_map/ppermute | solution.py:15
  186.4 5.7 %collective-permute-start.15 = (bf16[8,128,192]{1,2,0:T(8,128)(2,1)S(1)}, bf16[8,128,192]{1,2,0:T(8,128)(2,1)S(1)}, u32[]{:S(2)}, u32[]{:S(2)}) collective-permute-start(bf16[8,128,192]{1,2,0:T(8,128)(2,1)S(1)} %broadcast_multiply_fusion.1), channel_id=1, source_target_pairs={{16,0},{20,4},{24,8},{28,12},{32,16},{36,20},{40,24},{44,28},{48,3... | collective-permute-start | bytes 1179656 | tf_op jit(solution)/shard_map/ppermute | solution.py:15
  192.2 21.5 %collective-permute-done.11 = bf16[8,128,192]{1,2,0:T(8,128)(2,1)S(1)} collective-permute-done((bf16[8,128,192]{1,2,0:T(8,128)(2,1)S(1)}, bf16[8,128,192]{1,2,0:T(8,128)(2,1)S(1)}, u32[]{:S(2)}, u32[]{:S(2)}) %collective-permute-start.11) | collective-permute-done | bytes 393248 | tf_op jit(solution)/shard_map/ppermute | solution.py:15
  214.2 2.3 pad_maximum_fusion.1
  216.5 12.0 %gather_fusion.17 = bf16[192,128,192]{1,2,0:T(8,128)(2,1)} fusion(bf16[80,128,192]{1,2,0:T(8,128)(2,1)} %pad_maximum_fusion.1, s32[1024]{0:T(1024)S(1)} %pad_clamp_fusion), kind=kCustom, calls=%fused_computation.17 | custom fusion | bytes 18875136 | tf_op jit(solution)/shard_map/gather | solution.py:46
  228.5 15.8 %fusion.8 = bf16[192,128,192]{1,2,0:T(8,128)(2,1)} fusion(bf16[192,128,192]{1,2,0:T(8,128)(2,1)} %gather_fusion.17, bf16[192,128,128]{2,1,0:T(8,128)(2,1)} %param.11, bf16[192]{0:T(256)(128)(2,1)S(1)} %compare_convert_fusion.8), kind=kOutput, calls=%fused_computation.36 | convolution fusion | flops 1211105280 | bytes 25166208 | tf_op jit(solution)/shard_map/tij,tjf->tif/dot_general | solution.py:47
  244.3 8.8 %divide_convert_fusion.1 = bf16[16,128,192]{1,0,2:T(8,128)(2,1)S(1)} fusion(bf16[192,128,192]{1,2,0:T(8,128)(2,1)} %fusion.8, f32[16,128]{1,0:T(8,128)S(1)} %copy-done.3, s32[192]{0:T(256)S(1)} %copy-done.27), kind=kOutput, calls=%fused_computation.59 | convolution fusion | flops 151784448 | bytes 10232576 | tf_op jit(solution)/shard_map/bt,tif->bif/dot_general | solution.py:48
  255.2 2.9 fusion.33
  258.1 37.4 %all-gather.13.cloned.1.call-done = bf16[2048,768]{0,1:T(8,128)(2,1)} async-done(((bf16[2048,192]{0,1:T(8,128)(2,1)}), bf16[2048,768]{0,1:T(8,128)(2,1)}) %all-gather.13.cloned.1.call-update) | async-done | bytes 3145744 | tf_op jit(solution)/shard_map/all_gather | solution.py:61
  295.5 3.8 fusion.20
  299.4 1.3 copy_bitcast_fusion.3
  300.7 1.5 gather_fusion.18
  309.4 5.1 %collective-permute-start.17 = (bf16[8,128,192]{1,2,0:T(8,128)(2,1)S(1)}, bf16[8,128,192]{1,2,0:T(8,128)(2,1)S(1)}, u32[]{:S(2)}, u32[]{:S(2)}) collective-permute-start(bf16[8,128,192]{1,2,0:T(8,128)(2,1)S(1)} %broadcast_multiply_fusion.18), channel_id=1, source_target_pairs={{4,0},{8,4},{12,8},{16,12},{20,16},{24,20},{28,24},{32,28},{36,32}... | collective-permute-start | bytes 1179656 | tf_op jit(solution)/shard_map/ppermute | solution.py:15
  316.2 5.4 %collective-permute-start.19 = (bf16[8,128,192]{1,2,0:T(8,128)(2,1)S(1)}, bf16[8,128,192]{1,2,0:T(8,128)(2,1)S(1)}, u32[]{:S(2)}, u32[]{:S(2)}) collective-permute-start(bf16[8,128,192]{1,2,0:T(8,128)(2,1)S(1)} %broadcast_multiply_fusion.12), channel_id=1, source_target_pairs={{8,0},{12,4},{16,8},{20,12},{24,16},{28,20},{32,24},{36,28},{40,32... | collective-permute-start | bytes 1179656 | tf_op jit(solution)/shard_map/ppermute | solution.py:15
  323.3 5.4 %collective-permute-start.21 = (bf16[8,128,192]{1,2,0:T(8,128)(2,1)S(1)}, bf16[8,128,192]{1,2,0:T(8,128)(2,1)S(1)}, u32[]{:S(2)}, u32[]{:S(2)}) collective-permute-start(bf16[8,128,192]{1,2,0:T(8,128)(2,1)S(1)} %broadcast_multiply_fusion.6), channel_id=1, source_target_pairs={{12,0},{16,4},{20,8},{24,12},{28,16},{32,20},{36,24},{40,28},{44,3... | collective-permute-start | bytes 1179656 | tf_op jit(solution)/shard_map/ppermute | solution.py:15
  329.0 5.9 %collective-permute-start.23 = (bf16[8,128,192]{1,2,0:T(8,128)(2,1)S(1)}, bf16[8,128,192]{1,2,0:T(8,128)(2,1)S(1)}, u32[]{:S(2)}, u32[]{:S(2)}) collective-permute-start(bf16[8,128,192]{1,2,0:T(8,128)(2,1)S(1)} %broadcast_multiply_fusion), channel_id=1, source_target_pairs={{16,0},{20,4},{24,8},{28,12},{32,16},{36,20},{40,24},{44,28},{48,3... | collective-permute-start | bytes 1179656 | tf_op jit(solution)/shard_map/ppermute | solution.py:15
  335.0 21.3 %collective-permute-done.19 = bf16[8,128,192]{1,2,0:T(8,128)(2,1)S(1)} collective-permute-done((bf16[8,128,192]{1,2,0:T(8,128)(2,1)S(1)}, bf16[8,128,192]{1,2,0:T(8,128)(2,1)S(1)}, u32[]{:S(2)}, u32[]{:S(2)}) %collective-permute-start.19) | collective-permute-done | bytes 393248 | tf_op jit(solution)/shard_map/ppermute | solution.py:15
  356.6 2.3 pad_maximum_fusion.2
  358.9 11.8 %gather_fusion.26 = bf16[192,128,192]{1,2,0:T(8,128)(2,1)} fusion(bf16[80,128,192]{1,2,0:T(8,128)(2,1)} %pad_maximum_fusion.2, s32[1024]{0:T(1024)S(1)} %pad_clamp_fusion), kind=kCustom, calls=%fused_computation.26 | custom fusion | bytes 18875136 | tf_op jit(solution)/shard_map/gather | solution.py:46
  370.7 16.0 %fusion.6 = bf16[192,128,192]{1,2,0:T(8,128)(2,1)} fusion(bf16[192,128,192]{1,2,0:T(8,128)(2,1)} %gather_fusion.26, bf16[192,128,128]{2,1,0:T(8,128)(2,1)} %param.11, bf16[192]{0:T(256)(128)(2,1)S(1)} %compare_convert_fusion.8), kind=kOutput, calls=%fused_computation.34 | convolution fusion | flops 1211105280 | bytes 25166208 | tf_op jit(solution)/shard_map/tij,tjf->tif/dot_general | solution.py:47
  386.8 8.8 %divide_convert_fusion = bf16[16,128,192]{1,0,2:T(8,128)(2,1)S(1)} fusion(bf16[192,128,192]{1,2,0:T(8,128)(2,1)} %fusion.6, f32[16,128]{1,0:T(8,128)S(1)} %copy-done.3, s32[192]{0:T(256)S(1)} %copy-done.28), kind=kOutput, calls=%fused_computation.58 | convolution fusion | flops 151784448 | bytes 10232576 | tf_op jit(solution)/shard_map/bt,tif->bif/dot_general | solution.py:48
  397.4 2.9 fusion.30
  400.3 37.8 %all-gather.17.cloned.1.call-done = bf16[2048,768]{0,1:T(8,128)(2,1)} async-done(((bf16[2048,192]{0,1:T(8,128)(2,1)}), bf16[2048,768]{0,1:T(8,128)(2,1)}) %all-gather.17.cloned.1.call-update) | async-done | bytes 3145744 | tf_op jit(solution)/shard_map/all_gather | solution.py:61
  438.1 3.8 fusion.22
  (199 shorter events, 46.7 us)
Async XLA Ops:
  6.5 108.8 %all-gather.7.cloned.1.call-start = ((), (), s32[]{:S(2)}) async-start(), calls=%async_computation | async-start | bytes 3932160 | tf_op jit(solution)/shard_map/all_gather | solution.py:56
  7.3 146.5 %all-gather.9.cloned.1.call-start = ((), (), s32[]{:S(2)}) async-start(), calls=%async_computation.1 | async-start | bytes 3932160 | tf_op jit(solution)/shard_map/all_gather | solution.py:61
  11.9 9.4 %copy-start.12 = (bf16[8]{0:T(256)(128)(2,1)}, bf16[8]{0:T(256)(128)(2,1)S(1)}, u32[]{:S(2)}) copy-start(bf16[8]{0:T(256)(128)(2,1)S(1)} %compare_convert_fusion.7) | copy-start | bytes 52
  11.9 12.2 %copy-start.4 = (s32[1024]{0:T(1024)}, s32[1024]{0:T(1024)S(1)}, u32[]{:S(2)}) copy-start(s32[1024]{0:T(1024)S(1)} %get-tuple-element.36) | copy-start | bytes 12292
  11.9 12.2 %copy-start.5 = (s32[1024]{0:T(1024)}, s32[1024]{0:T(1024)S(1)}, u32[]{:S(2)}) copy-start(s32[1024]{0:T(1024)S(1)} %get-tuple-element.37) | copy-start | bytes 12292
  13.4 31.4 %collective-permute-start = (bf16[8,128,192]{1,2,0:T(8,128)(2,1)}, bf16[8,128,192]{1,2,0:T(8,128)(2,1)S(1)}, u32[]{:S(2)}, u32[]{:S(2)}) collective-permute-start(bf16[8,128,192]{1,2,0:T(8,128)(2,1)} %broadcast_multiply_fusion.23), channel_id=1, source_target_pairs={{124,0},{0,4},{4,8},{8,12},{12,16},{16,20},{20,24},{24,28},{28,32}... | collective-permute-start | bytes 1179656 | tf_op jit(solution)/shard_map/ppermute | solution.py:15
  14.6 6.7 %copy-start.14 = (bf16[8]{0:T(256)(128)(2,1)}, bf16[8]{0:T(256)(128)(2,1)S(1)}, u32[]{:S(2)}) copy-start(bf16[8]{0:T(256)(128)(2,1)S(1)} %compare_convert_fusion.6) | copy-start | bytes 52
  15.5 34.8 %collective-permute-start.1 = (bf16[8,128,192]{1,2,0:T(8,128)(2,1)}, bf16[8,128,192]{1,2,0:T(8,128)(2,1)S(1)}, u32[]{:S(2)}, u32[]{:S(2)}) collective-permute-start(bf16[8,128,192]{1,2,0:T(8,128)(2,1)} %broadcast_multiply_fusion.20), channel_id=1, source_target_pairs={{4,0},{8,4},{12,8},{16,12},{20,16},{24,20},{28,24},{32,28},{36,32}... | collective-permute-start | bytes 1179656 | tf_op jit(solution)/shard_map/ppermute | solution.py:15
  21.3 12.5 %copy-start.6 = (s32[1024]{0:T(1024)}, s32[1024]{0:T(1024)S(1)}, u32[]{:S(2)}) copy-start(s32[1024]{0:T(1024)S(1)} %get-tuple-element.34) | copy-start | bytes 12292
  21.3 12.5 %copy-start.7 = (s32[1024]{0:T(1024)}, s32[1024]{0:T(1024)S(1)}, u32[]{:S(2)}) copy-start(s32[1024]{0:T(1024)S(1)} %get-tuple-element.35) | copy-start | bytes 12292
  22.6 12.0 %copy-start.16 = (bf16[8]{0:T(256)(128)(2,1)}, bf16[8]{0:T(256)(128)(2,1)S(1)}, u32[]{:S(2)}) copy-start(bf16[8]{0:T(256)(128)(2,1)S(1)} %compare_convert_fusion.5) | copy-start | bytes 52
  23.5 27.0 %collective-permute-start.2 = (bf16[8,128,192]{1,2,0:T(8,128)(2,1)}, bf16[8,128,192]{1,2,0:T(8,128)(2,1)S(1)}, u32[]{:S(2)}, u32[]{:S(2)}) collective-permute-start(bf16[8,128,192]{1,2,0:T(8,128)(2,1)} %broadcast_multiply_fusion.17), channel_id=1, source_target_pairs={{120,0},{124,4},{0,8},{4,12},{8,16},{12,20},{16,24},{20,28},{24,32... | collective-permute-start | bytes 1179656 | tf_op jit(solution)/shard_map/ppermute | solution.py:15
  25.7 30.5 %collective-permute-start.3 = (bf16[8,128,192]{1,2,0:T(8,128)(2,1)}, bf16[8,128,192]{1,2,0:T(8,128)(2,1)S(1)}, u32[]{:S(2)}, u32[]{:S(2)}) collective-permute-start(bf16[8,128,192]{1,2,0:T(8,128)(2,1)} %broadcast_multiply_fusion.14), channel_id=1, source_target_pairs={{8,0},{12,4},{16,8},{20,12},{24,16},{28,20},{32,24},{36,28},{40,32... | collective-permute-start | bytes 1179656 | tf_op jit(solution)/shard_map/ppermute | solution.py:15
  33.2 23.1 %collective-permute-start.4 = (bf16[8,128,192]{1,2,0:T(8,128)(2,1)}, bf16[8,128,192]{1,2,0:T(8,128)(2,1)}, u32[]{:S(2)}, u32[]{:S(2)}) collective-permute-start(bf16[8,128,192]{1,2,0:T(8,128)(2,1)} %broadcast_multiply_fusion.11), channel_id=1, source_target_pairs={{116,0},{120,4},{124,8},{0,12},{4,16},{8,20},{12,24},{16,28},{20,3... | collective-permute-start | bytes 1179656 | tf_op jit(solution)/shard_map/ppermute | solution.py:15
  34.5 10.1 %copy-start.19 = (bf16[8]{0:T(256)(128)(2,1)}, bf16[8]{0:T(256)(128)(2,1)S(1)}, u32[]{:S(2)}) copy-start(bf16[8]{0:T(256)(128)(2,1)S(1)} %compare_convert_fusion.2) | copy-start | bytes 52
  37.2 7.4 %copy-start.23 = (bf16[8]{0:T(256)(128)(2,1)}, bf16[8]{0:T(256)(128)(2,1)S(1)}, u32[]{:S(2)}) copy-start(bf16[8]{0:T(256)(128)(2,1)S(1)} %compare_convert_fusion) | copy-start | bytes 52
  44.8 53.5 %copy-start.2 = (f32[16,128]{1,0:T(8,128)}, f32[16,128]{1,0:T(8,128)S(1)}, u32[]{:S(2)}) copy-start(f32[16,128]{1,0:T(8,128)S(1)} %convolution_add_fusion.3) | copy-start | bytes 24580
  44.8 14.9 %collective-permute-start.5 = (bf16[8,128,192]{1,2,0:T(8,128)(2,1)S(1)}, bf16[8,128,192]{1,2,0:T(8,128)(2,1)S(1)}, u32[]{:S(2)}, u32[]{:S(2)}) collective-permute-start(bf16[8,128,192]{1,2,0:T(8,128)(2,1)S(1)} %broadcast_multiply_fusion.8), channel_id=1, source_target_pairs={{12,0},{16,4},{20,8},{24,12},{28,16},{32,20},{36,24},{40,28},{44,3... | collective-permute-start | bytes 1179656 | tf_op jit(solution)/shard_map/ppermute | solution.py:15
  50.3 15.5 %collective-permute-start.6 = (bf16[8,128,192]{1,2,0:T(8,128)(2,1)S(1)}, bf16[8,128,192]{1,2,0:T(8,128)(2,1)S(1)}, u32[]{:S(2)}, u32[]{:S(2)}) collective-permute-start(bf16[8,128,192]{1,2,0:T(8,128)(2,1)S(1)} %broadcast_multiply_fusion.5), channel_id=1, source_target_pairs={{112,0},{116,4},{120,8},{124,12},{0,16},{4,20},{8,24},{12,28},{16,... | collective-permute-start | bytes 1179656 | tf_op jit(solution)/shard_map/ppermute | solution.py:15
  50.4 17.7 %collective-permute-start.7 = (bf16[8,128,192]{1,2,0:T(8,128)(2,1)S(1)}, bf16[8,128,192]{1,2,0:T(8,128)(2,1)S(1)}, u32[]{:S(2)}, u32[]{:S(2)}) collective-permute-start(bf16[8,128,192]{1,2,0:T(8,128)(2,1)S(1)} %broadcast_multiply_fusion.2), channel_id=1, source_target_pairs={{16,0},{20,4},{24,8},{28,12},{32,16},{36,20},{40,24},{44,28},{48,3... | collective-permute-start | bytes 1179656 | tf_op jit(solution)/shard_map/ppermute | solution.py:15
  98.3 12.0 %copy-start = (bf16[3,768,768]{2,1,0:T(8,128)(2,1)S(1)}, bf16[3,768,768]{2,1,0:T(8,128)(2,1)}, u32[]{:S(2)}) copy-start(bf16[3,768,768]{2,1,0:T(8,128)(2,1)} %param.17) | copy-start | bytes 10616836
  108.4 146.8 %all-gather.11.cloned.1.call-start = ((), (), s32[]{:S(2)}) async-start(), calls=%async_computation.2 | async-start | bytes 3932160 | tf_op jit(solution)/shard_map/all_gather | solution.py:56
  157.4 138.1 %all-gather.13.cloned.1.call-start = ((), (), s32[]{:S(2)}) async-start(), calls=%async_computation.3 | async-start | bytes 3932160 | tf_op jit(solution)/shard_map/all_gather | solution.py:61
  165.6 15.0 %copy-start.21 = (bf16[8]{0:T(256)(128)(2,1)S(1)}, bf16[8]{0:T(256)(128)(2,1)}, u32[]{:S(2)}) copy-start(bf16[8]{0:T(256)(128)(2,1)} %copy-done.20) | copy-start | bytes 52
  165.6 15.1 %copy-start.24 = (bf16[8]{0:T(256)(128)(2,1)S(1)}, bf16[8]{0:T(256)(128)(2,1)}, u32[]{:S(2)}) copy-start(bf16[8]{0:T(256)(128)(2,1)} %copy-done.23) | copy-start | bytes 52
  166.7 14.1 %collective-permute-start.8 = (bf16[8,128,192]{1,2,0:T(8,128)(2,1)S(1)}, bf16[8,128,192]{1,2,0:T(8,128)(2,1)S(1)}, u32[]{:S(2)}, u32[]{:S(2)}) collective-permute-start(bf16[8,128,192]{1,2,0:T(8,128)(2,1)S(1)} %broadcast_multiply_fusion.22), channel_id=1, source_target_pairs={{124,0},{0,4},{4,8},{8,12},{12,16},{16,20},{20,24},{24,28},{28,32}... | collective-permute-start | bytes 1179656 | tf_op jit(solution)/shard_map/ppermute | solution.py:15
  166.9 19.4 %collective-permute-start.9 = (bf16[8,128,192]{1,2,0:T(8,128)(2,1)S(1)}, bf16[8,128,192]{1,2,0:T(8,128)(2,1)S(1)}, u32[]{:S(2)}, u32[]{:S(2)}) collective-permute-start(bf16[8,128,192]{1,2,0:T(8,128)(2,1)S(1)} %broadcast_multiply_fusion.19), channel_id=1, source_target_pairs={{4,0},{8,4},{12,8},{16,12},{20,16},{24,20},{28,24},{32,28},{36,32}... | collective-permute-start | bytes 1179656 | tf_op jit(solution)/shard_map/ppermute | solution.py:15
  172.8 13.6 %collective-permute-start.10 = (bf16[8,128,192]{1,2,0:T(8,128)(2,1)S(1)}, bf16[8,128,192]{1,2,0:T(8,128)(2,1)S(1)}, u32[]{:S(2)}, u32[]{:S(2)}) collective-permute-start(bf16[8,128,192]{1,2,0:T(8,128)(2,1)S(1)} %broadcast_multiply_fusion.16), channel_id=1, source_target_pairs={{120,0},{124,4},{0,8},{4,12},{8,16},{12,20},{16,24},{20,28},{24,32... | collective-permute-start | bytes 1179656 | tf_op jit(solution)/shard_map/ppermute | solution.py:15
  173.7 40.0 %collective-permute-start.11 = (bf16[8,128,192]{1,2,0:T(8,128)(2,1)S(1)}, bf16[8,128,192]{1,2,0:T(8,128)(2,1)S(1)}, u32[]{:S(2)}, u32[]{:S(2)}) collective-permute-start(bf16[8,128,192]{1,2,0:T(8,128)(2,1)S(1)} %broadcast_multiply_fusion.13), channel_id=1, source_target_pairs={{8,0},{12,4},{16,8},{20,12},{24,16},{28,20},{32,24},{36,28},{40,32... | collective-permute-start | bytes 1179656 | tf_op jit(solution)/shard_map/ppermute | solution.py:15
  179.8 34.0 %collective-permute-start.12 = (bf16[8,128,192]{1,2,0:T(8,128)(2,1)S(1)}, bf16[8,128,192]{1,2,0:T(8,128)(2,1)S(1)}, u32[]{:S(2)}, u32[]{:S(2)}) collective-permute-start(bf16[8,128,192]{1,2,0:T(8,128)(2,1)S(1)} %broadcast_multiply_fusion.10), channel_id=1, source_target_pairs={{116,0},{120,4},{124,8},{0,12},{4,16},{8,20},{12,24},{16,28},{20,3... | collective-permute-start | bytes 1179656 | tf_op jit(solution)/shard_map/ppermute | solution.py:15
  180.8 33.0 %collective-permute-start.13 = (bf16[8,128,192]{1,2,0:T(8,128)(2,1)S(1)}, bf16[8,128,192]{1,2,0:T(8,128)(2,1)S(1)}, u32[]{:S(2)}, u32[]{:S(2)}) collective-permute-start(bf16[8,128,192]{1,2,0:T(8,128)(2,1)S(1)} %broadcast_multiply_fusion.7), channel_id=1, source_target_pairs={{12,0},{16,4},{20,8},{24,12},{28,16},{32,20},{36,24},{40,28},{44,3... | collective-permute-start | bytes 1179656 | tf_op jit(solution)/shard_map/ppermute | solution.py:15
  186.3 27.6 %collective-permute-start.14 = (bf16[8,128,192]{1,2,0:T(8,128)(2,1)S(1)}, bf16[8,128,192]{1,2,0:T(8,128)(2,1)S(1)}, u32[]{:S(2)}, u32[]{:S(2)}) collective-permute-start(bf16[8,128,192]{1,2,0:T(8,128)(2,1)S(1)} %broadcast_multiply_fusion.4), channel_id=1, source_target_pairs={{112,0},{116,4},{120,8},{124,12},{0,16},{4,20},{8,24},{12,28},{16,... | collective-permute-start | bytes 1179656 | tf_op jit(solution)/shard_map/ppermute | solution.py:15
  186.4 27.7 %collective-permute-start.15 = (bf16[8,128,192]{1,2,0:T(8,128)(2,1)S(1)}, bf16[8,128,192]{1,2,0:T(8,128)(2,1)S(1)}, u32[]{:S(2)}, u32[]{:S(2)}) collective-permute-start(bf16[8,128,192]{1,2,0:T(8,128)(2,1)S(1)} %broadcast_multiply_fusion.1), channel_id=1, source_target_pairs={{16,0},{20,4},{24,8},{28,12},{32,16},{36,20},{40,24},{44,28},{48,3... | collective-permute-start | bytes 1179656 | tf_op jit(solution)/shard_map/ppermute | solution.py:15
  228.5 15.8 %copy-start.3 = (f32[16,128]{1,0:T(8,128)S(1)}, f32[16,128]{1,0:T(8,128)}, u32[]{:S(2)}) copy-start(f32[16,128]{1,0:T(8,128)} %copy-done.2) | copy-start | bytes 24580
  228.5 15.8 %copy-start.27 = (s32[192]{0:T(256)S(1)}, s32[192]{0:T(256)}, u32[]{:S(2)}) copy-start(s32[192]{0:T(256)} %param.12) | copy-start | bytes 2308
  254.2 143.3 %all-gather.15.cloned.1.call-start = ((), (), s32[]{:S(2)}) async-start(), calls=%async_computation.4 | async-start | bytes 3932160 | tf_op jit(solution)/shard_map/all_gather | solution.py:56
  299.3 138.8 %all-gather.17.cloned.1.call-start = ((), (), s32[]{:S(2)}) async-start(), calls=%async_computation.5 | async-start | bytes 3932160 | tf_op jit(solution)/shard_map/all_gather | solution.py:61
  307.4 15.7 %copy-start.22 = (bf16[8]{0:T(256)(128)(2,1)S(1)}, bf16[8]{0:T(256)(128)(2,1)}, u32[]{:S(2)}) copy-start(bf16[8]{0:T(256)(128)(2,1)} %copy-done.20) | copy-start | bytes 52
  307.5 15.8 %copy-start.25 = (bf16[8]{0:T(256)(128)(2,1)S(1)}, bf16[8]{0:T(256)(128)(2,1)}, u32[]{:S(2)}) copy-start(bf16[8]{0:T(256)(128)(2,1)} %copy-done.23) | copy-start | bytes 52
  308.6 14.8 %collective-permute-start.16 = (bf16[8,128,192]{1,2,0:T(8,128)(2,1)S(1)}, bf16[8,128,192]{1,2,0:T(8,128)(2,1)S(1)}, u32[]{:S(2)}, u32[]{:S(2)}) collective-permute-start(bf16[8,128,192]{1,2,0:T(8,128)(2,1)S(1)} %broadcast_multiply_fusion.21), channel_id=1, source_target_pairs={{124,0},{0,4},{4,8},{8,12},{12,16},{16,20},{20,24},{24,28},{28,32}... | collective-permute-start | bytes 1179656 | tf_op jit(solution)/shard_map/ppermute | solution.py:15
  309.4 19.4 %collective-permute-start.17 = (bf16[8,128,192]{1,2,0:T(8,128)(2,1)S(1)}, bf16[8,128,192]{1,2,0:T(8,128)(2,1)S(1)}, u32[]{:S(2)}, u32[]{:S(2)}) collective-permute-start(bf16[8,128,192]{1,2,0:T(8,128)(2,1)S(1)} %broadcast_multiply_fusion.18), channel_id=1, source_target_pairs={{4,0},{8,4},{12,8},{16,12},{20,16},{24,20},{28,24},{32,28},{36,32}... | collective-permute-start | bytes 1179656 | tf_op jit(solution)/shard_map/ppermute | solution.py:15
  315.3 13.6 %collective-permute-start.18 = (bf16[8,128,192]{1,2,0:T(8,128)(2,1)S(1)}, bf16[8,128,192]{1,2,0:T(8,128)(2,1)S(1)}, u32[]{:S(2)}, u32[]{:S(2)}) collective-permute-start(bf16[8,128,192]{1,2,0:T(8,128)(2,1)S(1)} %broadcast_multiply_fusion.15), channel_id=1, source_target_pairs={{120,0},{124,4},{0,8},{4,12},{8,16},{12,20},{16,24},{20,28},{24,32... | collective-permute-start | bytes 1179656 | tf_op jit(solution)/shard_map/ppermute | solution.py:15
  316.2 40.0 %collective-permute-start.19 = (bf16[8,128,192]{1,2,0:T(8,128)(2,1)S(1)}, bf16[8,128,192]{1,2,0:T(8,128)(2,1)S(1)}, u32[]{:S(2)}, u32[]{:S(2)}) collective-permute-start(bf16[8,128,192]{1,2,0:T(8,128)(2,1)S(1)} %broadcast_multiply_fusion.12), channel_id=1, source_target_pairs={{8,0},{12,4},{16,8},{20,12},{24,16},{28,20},{32,24},{36,28},{40,32... | collective-permute-start | bytes 1179656 | tf_op jit(solution)/shard_map/ppermute | solution.py:15
  322.3 34.0 %collective-permute-start.20 = (bf16[8,128,192]{1,2,0:T(8,128)(2,1)S(1)}, bf16[8,128,192]{1,2,0:T(8,128)(2,1)S(1)}, u32[]{:S(2)}, u32[]{:S(2)}) collective-permute-start(bf16[8,128,192]{1,2,0:T(8,128)(2,1)S(1)} %broadcast_multiply_fusion.9), channel_id=1, source_target_pairs={{116,0},{120,4},{124,8},{0,12},{4,16},{8,20},{12,24},{16,28},{20,3... | collective-permute-start | bytes 1179656 | tf_op jit(solution)/shard_map/ppermute | solution.py:15
  323.3 33.0 %collective-permute-start.21 = (bf16[8,128,192]{1,2,0:T(8,128)(2,1)S(1)}, bf16[8,128,192]{1,2,0:T(8,128)(2,1)S(1)}, u32[]{:S(2)}, u32[]{:S(2)}) collective-permute-start(bf16[8,128,192]{1,2,0:T(8,128)(2,1)S(1)} %broadcast_multiply_fusion.6), channel_id=1, source_target_pairs={{12,0},{16,4},{20,8},{24,12},{28,16},{32,20},{36,24},{40,28},{44,3... | collective-permute-start | bytes 1179656 | tf_op jit(solution)/shard_map/ppermute | solution.py:15
  328.8 27.6 %collective-permute-start.22 = (bf16[8,128,192]{1,2,0:T(8,128)(2,1)S(1)}, bf16[8,128,192]{1,2,0:T(8,128)(2,1)S(1)}, u32[]{:S(2)}, u32[]{:S(2)}) collective-permute-start(bf16[8,128,192]{1,2,0:T(8,128)(2,1)S(1)} %broadcast_multiply_fusion.3), channel_id=1, source_target_pairs={{112,0},{116,4},{120,8},{124,12},{0,16},{4,20},{8,24},{12,28},{16,... | collective-permute-start | bytes 1179656 | tf_op jit(solution)/shard_map/ppermute | solution.py:15
  329.0 27.6 %collective-permute-start.23 = (bf16[8,128,192]{1,2,0:T(8,128)(2,1)S(1)}, bf16[8,128,192]{1,2,0:T(8,128)(2,1)S(1)}, u32[]{:S(2)}, u32[]{:S(2)}) collective-permute-start(bf16[8,128,192]{1,2,0:T(8,128)(2,1)S(1)} %broadcast_multiply_fusion), channel_id=1, source_target_pairs={{16,0},{20,4},{24,8},{28,12},{32,16},{36,20},{40,24},{44,28},{48,3... | collective-permute-start | bytes 1179656 | tf_op jit(solution)/shard_map/ppermute | solution.py:15
  370.7 16.0 %copy-start.28 = (s32[192]{0:T(256)S(1)}, s32[192]{0:T(256)}, u32[]{:S(2)}) copy-start(s32[192]{0:T(256)} %param.12) | copy-start | bytes 2308
  (12 other events, 48.2 us)
Sparse Core Ops, SparseCore 0:
  9.0 41.9 all-gather.6
  108.5 45.1 all-gather.8
  157.5 39.6 all-gather.10
  254.3 41.1 all-gather.12
  299.4 39.6 all-gather.14
  396.8 41.2 all-gather.16
where the time goes:
time: 458 us; the launch traced here: 449 us
  waiting for transfers between devices  165 us (36%)
  matrix products  94.1 us (21%)
  local copies, waits for them, and re-layouts  73.4 us (16%)
  starting transfers between devices  67.2 us (15%)
  other arithmetic  33.6 us (7%)
  between operations  15.8 us (3%)
    all_gather x3, waiting for transfers between devices, per_device(): lax.all_gather(agg, 'feat', axis=1, tiled=True)  111 us
    ppermute x24, starting transfers between devices, from_behind(): return lax.ppermute(block, axis, route)  66.4 us
    ppermute x24, waiting for transfers between devices, from_behind(): return lax.ppermute(block, axis, route)  53.7 us
    dot_general x3, matrix products, per_device(): jnp.einsum('tij,tjf->tif', masked, picked, preferred_element_type=jnp.flo...  47.5 us
    gather x3, local copies, waits for them, and re-layouts, per_device(): picked = source_list[tile_src]  35.8 us
    dot_general x3, matrix products, per_device(): jnp.einsum('bt,tif->bif', onehot, contrib, preferred_element_type=jnp.flo...  26.5 us
    gather x24, local copies, waits for them, and re-layouts, per_device(): outgoing.append(blocks_here[send_blocks[0, d]] * filled[:, None, None])  18.4 us
    mul x24, other arithmetic, per_device(): outgoing.append(blocks_here[send_blocks[0, d]] * filled[:, None, None])  14 us
  transfers between devices with their start and end apart: 30, of which 9 were waited for; matrix products, arithmetic and copies ran while one was open for 42% of the time, Pallas kernels for 0%

commit v1 on v0

v1 whole, which is shorter than its diff:
```python
import functools

import jax
import jax.numpy as jnp
from jax import lax
from jax.experimental import pallas as pl
from jax.experimental.pallas import tpu as pltpu
from jax.sharding import PartitionSpec as P

LAYERS = 3
BLK = 128
PEERS = 8
SLOTS = 8
MESH = pl.DeviceIdType.MESH
LANES = 128
PACK = 192
HEAD = 16
NC = 4
PLACES = 9
VMEM_BYTES = 60 * 1024 * 1024


def offset(d):
    return (d // 2 + 1) * (1 if d % 2 == 0 else -1)


def exchange(h_ref, tab_ref, w_ref, b_ref, g_ref, s_ref, held, own, lhs, load_sem, keep_sem, tab_sem,
             ysend, yrecv, xsend, xrecv, psend, precv):
    i = lax.axis_index("dom")
    y = lax.axis_index("feat")
    n_dom = lax.axis_size("dom")
    core = lax.rem(i, 2)
    y_up, y_down = lax.rem(y + 1, 4), lax.rem(y + 3, 4)
    x_up, x_down = lax.rem(i + 2, n_dom), lax.rem(i + n_dom - 2, n_dom)
    partner = i + 1 - 2 * core
    rows = h_ref.shape[0] // NC
    half = rows // 2
    blocks = rows // PACK

    def hrows(n, part=None):
        if part is None:
            return pl.ds(n * rows, rows)
        return pl.ds(n * rows + part * half, half)

    def grows(n):
        return pl.ds(0, HEAD + rows) if n == 0 else pl.ds(HEAD + n * rows, rows)

    def remote(src, dst, send, recv, dom, feat):
        return pltpu.make_async_remote_copy(
            src_ref=src, dst_ref=dst, send_sem=send, recv_sem=recv,
            device_id=(dom, feat), device_id_type=MESH)

    loads = [pltpu.make_async_copy(h_ref.at[hrows(n)], held.at[y, hrows(n)], load_sem.at[n]) for n in range(NC)]
    for load in loads:
        load.start()
    tab_load = pltpu.make_async_copy(tab_ref, own.at[pl.ds(0, HEAD)], tab_sem)
    tab_load.start()

    barrier = pltpu.get_barrier_semaphore()
    for dom, feat in ((i, y_up), (i, y_down), (x_up, y), (x_down, y), (partner, y)):
        pl.semaphore_signal(barrier, inc=1, device_id=(dom, feat), device_id_type=MESH)
    pl.semaphore_wait(barrier, 5)

    sent = []
    up, down = [], []
    for n in range(NC):
        loads[n].wait()
        a = remote(held.at[y, hrows(n)], held.at[y, hrows(n)], ysend.at[0, n], yrecv.at[0, n], i, y_up)
        b = remote(held.at[y, hrows(n)], held.at[y, hrows(n)], ysend.at[1, n], yrecv.at[1, n], i, y_down)
        a.start()
        b.start()
        up.append(a)
        down.append(b)
        sent += [a, b]

    def gather_relay(n):
        up[n].wait_recv()
        a = remote(held.at[y_down, hrows(n, 0)], held.at[y_down, hrows(n, 0)], ysend.at[2, n], yrecv.at[2, n], i, y_up)
        a.start()
        down[n].wait_recv()
        b = remote(held.at[y_up, hrows(n, 1)], held.at[y_up, hrows(n, 1)], ysend.at[3, n], yrecv.at[3, n], i, y_down)
        b.start()
        sent.extend([a, b])
        return a, b

    lane = lax.broadcasted_iota(jnp.int32, (64, LANES), 1)
    low = lane < 64

    def project(n):
        for j in range(blocks):
            base = n * rows + j * PACK
            out = slice(j * BLK, (j + 1) * BLK)
            top = slice(j * BLK, j * BLK + 64)
            bot = slice(j * BLK + 64, (j + 1) * BLK)
            for a in range(4):
                lhs[out, a * LANES:(a + 1) * LANES] = held[a, base:base + BLK, :]
            for pair in range(2):
                p0 = held[2 * pair, base + BLK:base + PACK, :]
                p1 = held[2 * pair + 1, base + BLK:base + PACK, :]
                cols = slice(512 + pair * LANES, 512 + (pair + 1) * LANES)
                lhs[top, cols] = jnp.concatenate([p0[:, :64], p1[:, :64]], axis=1)
                lhs[bot, cols] = jnp.concatenate([p0[:, 64:], p1[:, 64:]], axis=1)
        res = jnp.dot(lhs[...], w_ref[...], preferred_element_type=jnp.float32) + b_ref[...]
        for j in range(blocks):
            r0 = j * BLK
            base = n * rows + j * PACK
            own[HEAD + base:HEAD + base + BLK, :] = res[r0:r0 + BLK, :LANES].astype(jnp.bfloat16)
            s_ref[base:base + BLK, :] = res[r0:r0 + BLK, LANES:2 * LANES]
            top = res[r0:r0 + 64, 2 * LANES:]
            bot = res[r0 + 64:r0 + BLK, 2 * LANES:]
            own[HEAD + base + BLK:HEAD + base + PACK, :] = jnp.where(
                low, top, pltpu.roll(bot, 64, 1)).astype(jnp.bfloat16)
            s_ref[base + BLK:base + PACK, :] = jnp.where(low, pltpu.roll(top, 64, 1), bot)

    ours, first, second = [], [], []

    def send_own(n):
        src = own.at[grows(n)]
        keep = pltpu.make_async_copy(src, g_ref.at[4, grows(n)], keep_sem.at[n])
        a = remote(src, g_ref.at[2, grows(n)], xsend.at[0, n], xrecv.at[0, n], x_up, y)
        b = remote(src, g_ref.at[6, grows(n)], xsend.at[1, n], xrecv.at[1, n], x_down, y)
        c = remote(src, g_ref.at[3 + 2 * core, grows(n)], psend.at[0, n], precv.at[0, n], partner, y)
        for copy in (a, b, c, keep):
            copy.start()
        ours.append((a, b, c, keep))
        sent.extend([a, b, c])

    def relay_one(n):
        a, b, _, _ = ours[n]
        a.wait_recv()
        u = remote(g_ref.at[2, grows(n)], g_ref.at[0, grows(n)], xsend.at[2, n], xrecv.at[2, n], x_up, y)
        pu = remote(g_ref.at[2, grows(n)], g_ref.at[1 + 2 * core, grows(n)], psend.at[1, n], precv.at[1, n], partner, y)
        u.start()
        pu.start()
        b.wait_recv()
        v = remote(g_ref.at[6, grows(n)], g_ref.at[8, grows(n)], xsend.at[3, n], xrecv.at[3, n], x_down, y)
        pv = remote(g_ref.at[6, grows(n)], g_ref.at[5 + 2 * core, grows(n)], psend.at[2, n], precv.at[2, n], partner, y)
        v.start()
        pv.start()
        first.append((u, v, pu, pv))
        sent.extend([u, v, pu, pv])

    def relay_two(n):
        u, v, _, _ = first[n]
        u.wait_recv()
        v.wait_recv()
        c = remote(g_ref.at[8 - 8 * core, grows(n)], g_ref.at[7 - 6 * core, grows(n)], psend.at[3, n], precv.at[3, n],
                   partner, y)
        c.start()
        second.append(c)
        sent.append(c)

    tab_load.wait()
    for n in range(NC):
        a, b = gather_relay(n)
        a.wait_recv()
        b.wait_recv()
        project(n)
        send_own(n)
        if n >= 1:
            relay_one(n - 1)
        if n >= 2:
            relay_two(n - 2)
    relay_one(NC - 1)
    for n in range(max(NC - 2, 0), NC):
        relay_two(n)
    for n in range(NC):
        ours[n][2].wait_recv()
        first[n][2].wait_recv()
        first[n][3].wait_recv()
        second[n].wait_recv()
        ours[n][3].wait()
    for copy in sent:
        copy.wait_send()


def aggregate(last, tidx, roff, starts, g_ref, t_ref, s_ref, out_ref, gv, tv, g_sem, t_sem):
    slot_rows = g_ref.shape[1]
    tiles = t_ref.shape[0]
    groups = 4
    per = tiles // groups
    copies = [
        pltpu.make_async_copy(g_ref.at[p], gv.at[pl.ds(p * slot_rows, slot_rows)], g_sem.at[p])
        for p in range(PLACES)
    ] + [
        pltpu.make_async_copy(t_ref.at[pl.ds(k * per, per)], tv.at[pl.ds(k * per, per)], t_sem.at[k])
        for k in range(groups)
    ]
    for copy in copies:
        copy.start()
    gv[PLACES * slot_rows:PLACES * slot_rows + PACK, :] = jnp.zeros((PACK, LANES), jnp.bfloat16)
    tv[tiles] = jnp.zeros((BLK, BLK), jnp.bfloat16)
    for copy in copies:
        copy.wait()
    lane = lax.broadcasted_iota(jnp.int32, (64, LANES), 1)
    low = lane < 64
    ones = jnp.ones((64, 64), jnp.bfloat16)

    def source(q):
        row = pl.multiple_of(roff[q], 16)
        left = gv[pl.ds(row, BLK), :]
        pack = gv[pl.ds(row + BLK, 64), :]
        right = jnp.concatenate([
            jnp.concatenate([pack[:, :64], ones], axis=1),
            jnp.concatenate([pack[:, 64:], ones], axis=1),
        ], axis=0)
        return jnp.concatenate([left, right], axis=1)

    def block(b, carry):
        def pair(p, acc):
            q = 2 * p
            lhs = jnp.concatenate([tv[tidx[q]], tv[tidx[q + 1]]], axis=1)
            rhs = jnp.concatenate([source(q), source(q + 1)], axis=0)
            return acc + jnp.dot(lhs, rhs, preferred_element_type=jnp.float32)

        acc = lax.fori_loop(starts[b], starts[b + 1], pair, jnp.zeros((BLK, 2 * LANES), jnp.float32))
        scale = 1.0 / (1.0 + acc[:, PACK:PACK + 1])
        left = acc[:, :LANES] * scale
        right = acc[:, LANES:] * scale
        pack = jnp.where(low, right[:64], pltpu.roll(right[64:], 64, 1))
        base = pl.multiple_of(b * PACK, PACK)
        left = left + s_ref[pl.ds(base, BLK), :]
        pack = pack + s_ref[pl.ds(base + BLK, 64), :]
        if last:
            row = pl.multiple_of(b * BLK, BLK)
            out_ref[pl.ds(row, BLK), :LANES] = left.astype(jnp.bfloat16)
            out_ref[pl.ds(row, 64), LANES:] = pack[:, :64].astype(jnp.bfloat16)
            out_ref[pl.ds(row + 64, 64), LANES:] = pltpu.roll(pack, 64, 1)[:, :64].astype(jnp.bfloat16)
        else:
            out_ref[pl.ds(base, BLK), :] = jnp.maximum(left, 0.0).astype(jnp.bfloat16)
            out_ref[pl.ds(base + BLK, 64), :] = jnp.maximum(pack, 0.0).astype(jnp.bfloat16)
        return carry

    lax.fori_loop(0, s_ref.shape[0] // PACK, block, 0)


def per_device(
    feats, tile_vals, tile_dst, tile_src, tile_count, send_blocks, send_count, w_self, w_nbr, bias
):
    node_rows, cols = feats.shape
    blk_dev = node_rows // BLK
    packed_rows = blk_dev * PACK
    slot_rows = HEAD + packed_rows
    zero_row = PLACES * slot_rows
    tiles = tile_vals.shape[0]
    entries = tiles + blk_dev
    y = lax.axis_index("feat")
    i32 = jnp.int32

    def cut(w):
        here = lax.dynamic_slice_in_dim(w, y * cols, cols, 2)
        return here.reshape(LAYERS, 4, cols, cols)

    ws, wn = cut(w_self), cut(w_nbr)
    w = jnp.concatenate([wn[..., :128], ws[..., :128], wn[..., 128:], ws[..., 128:]], axis=3)
    w = jnp.concatenate(
        [w[:, :, :128].reshape(LAYERS, 512, 384), w[:, :, 128:].reshape(LAYERS, 256, 384)], axis=1
    )
    bias_here = lax.dynamic_slice_in_dim(bias, y * cols, cols, 1)
    b_all = jnp.concatenate(
        [jnp.zeros((LAYERS, 128)), bias_here[:, :128], jnp.zeros((LAYERS, 64)), bias_here[:, 128:]], axis=1
    ).astype(jnp.float32)[:, None, :]

    f3 = feats.reshape(blk_dev, BLK, cols)
    hidden = jnp.concatenate(
        [f3[..., :128], jnp.concatenate([f3[:, :64, 128:], f3[:, 64:, 128:]], axis=2)], axis=1
    ).reshape(packed_rows, LANES)

    table = jnp.zeros((HEAD, LANES), jnp.bfloat16)
    table = table.at[:PEERS, :SLOTS].set(send_blocks[0].astype(jnp.bfloat16))
    table = table.at[:PEERS, SLOTS].set(send_count[0].astype(jnp.bfloat16))

    ids = jnp.arange(tiles, dtype=i32)
    live = ids < tile_count[0]
    dsts = jnp.arange(blk_dev, dtype=i32)
    hits = (tile_dst[None, :] == dsts[:, None]) & live[None, :]
    pairs = (jnp.sum(hits.astype(i32), axis=1) + 1) // 2
    starts = jnp.sum(jnp.where(dsts[None, :] < jnp.arange(blk_dev + 1, dtype=i32)[:, None], pairs[None, :], 0), axis=1)
    before = jnp.sum(jnp.where(dsts[None, :] < tile_dst[:, None], pairs[None, :], 0), axis=1)
    rank = jnp.sum(
        ((tile_dst[None, :] == tile_dst[:, None]) & (ids[None, :] < ids[:, None])).astype(i32), axis=1
    )
    place = jnp.where(live, 2 * before + rank, -1)
    here = place[None, :] == jnp.arange(entries, dtype=i32)[:, None]
    tidx = jnp.sum(jnp.where(here, ids[None, :] - tiles, 0), axis=1) + tiles
    sidx = jnp.sum(jnp.where(here, tile_src[None, :] + 1, 0), axis=1) - 1

    exchange_call = pl.pallas_call(
        exchange,
        out_shape=(
            jax.ShapeDtypeStruct((PLACES, slot_rows, LANES), jnp.bfloat16),
            jax.ShapeDtypeStruct((packed_rows, LANES), jnp.float32),
        ),
        in_specs=[
            pl.BlockSpec(memory_space=pl.ANY),
            pl.BlockSpec(memory_space=pl.ANY),
            pl.BlockSpec(memory_space=pltpu.VMEM),
            pl.BlockSpec(memory_space=pltpu.VMEM),
        ],
        out_specs=(pl.BlockSpec(memory_space=pl.ANY), pl.BlockSpec(memory_space=pltpu.VMEM)),
        scratch_shapes=[
            pltpu.VMEM((4, packed_rows, LANES), jnp.bfloat16),
            pltpu.VMEM((slot_rows, LANES), jnp.bfloat16),
            pltpu.VMEM((node_rows // NC, 768), jnp.bfloat16),
            pltpu.SemaphoreType.DMA((NC,)),
            pltpu.SemaphoreType.DMA((NC,)),
            pltpu.SemaphoreType.DMA,
            pltpu.SemaphoreType.DMA((4, NC)),
            pltpu.SemaphoreType.DMA((4, NC)),
            pltpu.SemaphoreType.DMA((4, NC)),
            pltpu.SemaphoreType.DMA((4, NC)),
            pltpu.SemaphoreType.DMA((4, NC)),
            pltpu.SemaphoreType.DMA((4, NC)),
        ],
        compiler_params=pltpu.CompilerParams(
            collective_id=0, has_side_effects=True, vmem_limit_bytes=VMEM_BYTES
        ),
        name="exchange",
    )

    def aggregate_call(last):
        out = (node_rows, cols) if last else (packed_rows, LANES)
        return pl.pallas_call(
            functools.partial(aggregate, last),
            out_shape=jax.ShapeDtypeStruct(out, jnp.bfloat16),
            grid_spec=pltpu.PrefetchScalarGridSpec(
                num_scalar_prefetch=3,
                grid=(),
                in_specs=[
                    pl.BlockSpec(memory_space=pl.ANY),
                    pl.BlockSpec(memory_space=pl.ANY),
                    pl.BlockSpec(memory_space=pltpu.VMEM),
                ],
                out_specs=pl.BlockSpec(memory_space=pltpu.VMEM),
                scratch_shapes=[
                    pltpu.VMEM((zero_row + PACK, LANES), jnp.bfloat16),
                    pltpu.VMEM((tiles + 1, BLK, BLK), jnp.bfloat16),
                    pltpu.SemaphoreType.DMA((PLACES,)),
                    pltpu.SemaphoreType.DMA((4,)),
                ],
            ),
            compiler_params=pltpu.CompilerParams(vmem_limit_bytes=VMEM_BYTES),
            name="aggregate_last" if last else "aggregate",
        )

    roff = None
    for layer in range(LAYERS):
        g, s = exchange_call(hidden, table, w[layer], b_all[layer])
        if layer == 0:
            spots = [4 - offset(d) for d in range(PEERS)]
            pick = (jnp.arange(PLACES)[:, None] == jnp.array(spots)[None, :]).astype(jnp.float32)
            heads = jnp.sum(g[:, :PEERS, :16].astype(jnp.float32) * pick[:, :, None], axis=0).astype(i32)
            filled = jnp.arange(SLOTS, dtype=i32)[None, :] < heads[:, SLOTS:SLOTS + 1]
            spot_rows = jnp.array(spots, i32)[:, None] * slot_rows + HEAD
            theirs = jnp.where(filled, spot_rows + PACK * heads[:, :SLOTS], zero_row).reshape(-1)
            mine = 4 * slot_rows + HEAD + PACK * dsts
            rows = jnp.concatenate([mine, theirs])
            srcs = jnp.arange(rows.shape[0], dtype=i32)
            roff = jnp.sum(jnp.where(sidx[:, None] == srcs[None, :], rows[None, :] - zero_row, 0), axis=1) + zero_row
        hidden = aggregate_call(layer == LAYERS - 1)(tidx, roff, starts, g, tile_vals, s)
    return hidden


def solution(mesh):
    in_specs = (
        P("dom", "feat"),
        P("dom", None, None),
        P("dom"),
        P("dom"),
        P("dom"),
        P("dom", None, None),
        P("dom", None),
        P(),
        P(),
        P(),
    )
    out_specs = P("dom", "feat")
    return jax.shard_map(
        per_device, mesh=mesh, in_specs=in_specs, out_specs=out_specs, check_vma=False
    )
```

time: 458 us -> 318 us (0.69); the launches traced: 449 us -> 314 us
  Pallas kernels: 0 us -> 294 us
  waiting for transfers between devices: 165 us -> 0 us
  matrix products: 94.1 us -> 0 us
  starting transfers between devices: 67.2 us -> 0 us
  local copies, waits for them, and re-layouts: 73.4 us -> 10.2 us
  other arithmetic: 33.6 us -> 9.47 us
  between operations: 15.8 us -> 0.99 us
    pallas_call x0 -> x6, Pallas kernels: none -> 294 us  [the longest x3 198 us: per_device(): g, s = exchange_call(hidden, table, w[layer], b_all[layer])]
    all_gather x6 -> x0, waiting for transfers between devices: 111 us -> none  [the longest x3 111 us: per_device(): lax.all_gather(agg, 'feat', axis=1, tiled=True)]
    dot_general x13 -> x0, matrix products: 94.1 us -> none  [the longest x3 47.5 us: per_device(): jnp.einsum('tij,tjf->tif', masked, picked, preferred_element_type=jnp.flo...]
    ppermute x24 -> x0, starting transfers between devices: 66.4 us -> none  [from_behind(): return lax.ppermute(block, axis, route)]
    gather x27 -> x0, local copies, waits for them, and re-layouts: 54.2 us -> none  [the longest x3 35.8 us: per_device(): picked = source_list[tile_src]]
    ppermute x24 -> x0, waiting for transfers between devices: 53.7 us -> none  [from_behind(): return lax.ppermute(block, axis, route)]
    mul x24 -> x0, other arithmetic: 14 us -> none  [per_device(): outgoing.append(blocks_here[send_blocks[0, d]] * filled[:, None, None])]
    unnamed x84 -> x20, local copies, waits for them, and re-layouts: 6.8 us -> 0.06 us
  transfers between devices with their start and end apart: 30 -> 0, of which waited for: 9 -> 0; matrix products, arithmetic and copies ran while one was open for 42% -> 0% of each run, Pallas kernels for 0% -> 0%
where the time goes in v1:
time: 318 us; the launch traced here: 314 us
  Pallas kernels  294 us (92%)
  local copies, waits for them, and re-layouts  10.2 us (3%)
  other arithmetic  9.47 us (3%)
    pallas_call x3, Pallas kernels, per_device(): g, s = exchange_call(hidden, table, w[layer], b_all[layer])  198 us
    pallas_call x3, Pallas kernels, per_device(): aggregate_call(layer == LAYERS - 1)(tidx, roff, starts, g, tile_vals, s)  96.1 us

profile of v1, /device:TPU:0, one launch (start us, length us, event | category | flops | bytes accessed | tf_op | source)
XLA Modules:
  0.0 314.4 jit_solution(3915995654267940601)
XLA Ops:
  0.0 3.2 %constant_dynamic-slice_fusion.1 = (bf16[3,768,192]{2,1,0:T(8,128)(2,1)S(1)}, bf16[3,768,192]{2,1,0:T(8,128)(2,1)S(1)}) fusion(bf16[3,768,768]{2,1,0:T(8,128)(2,1)} %param.23, s32[]{:T(128)S(6)} %select_n.50, bf16[3,768,768]{2,1,0:T(8,128)(2,1)} %param.24), kind=kLoop, calls=%fused_computation.45 | loop fusion | bytes 3538948 | tf_op jit(solution)/shard_map/dynamic_slice | solution.py:251
  3.2 0.1 slice.130
  3.3 0.1 slice.131
  3.4 0.1 slice.132
  3.6 0.1 slice.133
  3.7 0.5 pad_maximum_fusion
  4.2 0.1 slice.134
  4.3 0.2 pad_maximum_fusion.2
  4.4 0.0 copy-start.4
  4.4 0.0 copy-start.8
  4.5 0.0 copy-start.9
  4.5 0.0 copy-start.1
  4.5 1.4 fusion.4
  5.9 0.1 constant_dynamic-slice_fusion
  5.9 0.1 constant_dynamic-slice_fusion.3
  6.0 0.1 pad_maximum_fusion.3
  6.1 0.6 fusion.9
  6.7 0.6 fusion.10
  7.3 0.1 copy.26
  7.4 0.7 and_reduce_fusion
  8.1 2.1 dynamic-slice_select_fusion
  10.2 1.8 scatter.9.tab_ref
  12.0 0.5 copy.28
  12.6 0.1 fusion.8
  12.7 0.1 slice.127
  12.8 0.0 copy-start.7
  12.8 0.0 copy-start.6
  12.8 1.1 maximum_maximum_fusion
  13.9 68.8 %exchange.3 = (bf16[9,3088,128]{2,1,0:T(8,128)(2,1)}, f32[3072,128]{1,0:T(8,128)}) custom-call(bf16[3072,128]{1,0:T(8,128)(2,1)} %bitcast.28, bf16[16,128]{1,0:T(8,128)(2,1)} %copy-done.2, bf16[768,384]{1,0:T(8,128)(2,1)} %get-tuple-element.44.w_ref, f32[1,384]{1,0:T(1,128)} %get-tuple-element.50.b_ref), custom_call_target="tpu_custom_call" | custom-call | tf_op jit(solution)/shard_map/exchange/pallas_call | solution.py:348
  82.7 0.8 multiply_reduce_fusion
  83.5 0.2 slice_reduce_fusion
  83.7 0.1 add_select_fusion
  83.8 0.1 concatenate.33
  83.9 0.1 add_add_fusion
  84.6 0.1 convert_reduce_fusion.1
  84.8 0.1 select_reduce_fusion.3
  84.9 0.2 convert_reduce_fusion
  85.1 0.2 select_reduce_fusion
  85.2 0.6 broadcast_add_fusion.1
  85.8 0.1 select_reduce_fusion.2
  85.9 0.6 broadcast_add_fusion.roff
  86.5 0.7 select_reduce_fusion.4.starts
  87.2 31.6 %aggregate.2.h_ref = bf16[3072,128]{1,0:T(8,128)(2,1)} custom-call(s32[208]{0:T(256)} %get-tuple-element.54.tidx, s32[208]{0:T(256)} %broadcast_add_fusion.roff, s32[17]{0:T(128)} %select_reduce_fusion.4.starts, bf16[9,3088,128]{2,1,0:T(8,128)(2,1)} %get-tuple-element.35.g_ref, bf16[192,128,128]{2,1,0:T(8,128)(2,1)} %t_ref.5, ...), custom_call_target="tpu_custom_call" | custom-call | tf_op jit(solution)/shard_map/aggregate/pallas_call | solution.py:360
  118.8 64.1 %exchange.4 = (bf16[9,3088,128]{2,1,0:T(8,128)(2,1)}, f32[3072,128]{1,0:T(8,128)}) custom-call(bf16[3072,128]{1,0:T(8,128)(2,1)} %aggregate.2.h_ref, bf16[16,128]{1,0:T(8,128)(2,1)} %copy-done.2, bf16[768,384]{1,0:T(8,128)(2,1)} %get-tuple-element.45.w_ref, f32[1,384]{1,0:T(1,128)} %get-tuple-element.49.b_ref), custom_call_target="tpu_custom_call" | custom-call | tf_op jit(solution)/shard_map/exchange/pallas_call | solution.py:348
  182.9 31.6 %aggregate.3.h_ref = bf16[3072,128]{1,0:T(8,128)(2,1)} custom-call(s32[208]{0:T(256)} %get-tuple-element.54.tidx, s32[208]{0:T(256)} %broadcast_add_fusion.roff, s32[17]{0:T(128)} %select_reduce_fusion.4.starts, bf16[9,3088,128]{2,1,0:T(8,128)(2,1)} %get-tuple-element.37.g_ref, bf16[192,128,128]{2,1,0:T(8,128)(2,1)} %t_ref.5, ...), custom_call_target="tpu_custom_call" | custom-call | tf_op jit(solution)/shard_map/aggregate/pallas_call | solution.py:360
  214.5 64.8 %exchange.5 = (bf16[9,3088,128]{2,1,0:T(8,128)(2,1)}, f32[3072,128]{1,0:T(8,128)}) custom-call(bf16[3072,128]{1,0:T(8,128)(2,1)} %aggregate.3.h_ref, bf16[16,128]{1,0:T(8,128)(2,1)} %copy-done.2, bf16[768,384]{1,0:T(8,128)(2,1)} %get-tuple-element.43.w_ref, f32[1,384]{1,0:T(1,128)} %get-tuple-element.48.b_ref), custom_call_target="tpu_custom_call" | custom-call | tf_op jit(solution)/shard_map/exchange/pallas_call | solution.py:348
  279.3 32.9 %aggregate_last.1 = bf16[2048,192]{1,0:T(8,128)(2,1)} custom-call(s32[208]{0:T(256)} %get-tuple-element.54.tidx, s32[208]{0:T(256)} %broadcast_add_fusion.roff, s32[17]{0:T(128)} %select_reduce_fusion.4.starts, bf16[9,3088,128]{2,1,0:T(8,128)(2,1)} %get-tuple-element.39.g_ref, bf16[192,128,128]{2,1,0:T(8,128)(2,1)} %t_ref.5, f32[3072,128]{1,0:T(8,128)} %get-tuple-element.40.s_ref), custom_call_target="tpu_custom_call" | custom-call | tf_op jit(solution)/shard_map/aggregate_last/pallas_call | solution.py:360
  312.2 2.2 copy.27
  (30 shorter events, 0.1 us)
Async XLA Ops:
  0.0 5.8 %copy-start = (f32[3,768]{1,0:T(4,128)S(1)}, f32[3,768]{1,0:T(4,128)}, u32[]{:S(2)}) copy-start(f32[3,768]{1,0:T(4,128)} %param.25) | copy-start | bytes 27652
  4.4 2.9 copy-start.4
  4.4 2.8 copy-start.8
  4.5 2.9 copy-start.9
  4.5 7.6 %copy-start.1 = (bf16[2048,192]{0,1:T(8,128)(2,1)S(1)}, bf16[2048,192]{0,1:T(8,128)(2,1)}, u32[]{:S(2)}) copy-start(bf16[2048,192]{0,1:T(8,128)(2,1)} %param.16) | copy-start | bytes 2359300
  12.0 0.7 copy-start.2
  12.8 69.9 %copy-start.7 = (s32[8]{0:T(128)S(1)}, s32[8]{0:T(128)}, u32[]{:S(2)}) copy-start(s32[8]{0:T(128)} %constant.104.clone) | copy-start | bytes 100
  12.8 70.9 %copy-start.6 = (s32[8]{0:T(128)S(1)}, s32[8]{0:T(128)}, u32[]{:S(2)}) copy-start(s32[8]{0:T(128)} %constant.111) | copy-start | bytes 100
  12.8 71.8 %copy-start.3 = (s32[192]{0:T(256)S(1)}, s32[192]{0:T(256)}, u32[]{:S(2)}) copy-start(s32[192]{0:T(256)} %param.18) | copy-start | bytes 2308
  12.8 72.2 %copy-start.5 = (s32[192]{0:T(256)S(1)}, s32[192]{0:T(256)}, u32[]{:S(2)}) copy-start(s32[192]{0:T(256)} %param.19) | copy-start | bytes 2308

commit v2 on v1

--- a/solution.py
+++ b/solution.py
@@ -15,8 +15,10 @@
 LANES = 128
 PACK = 192
 HEAD = 16
-NC = 4
+CHUNKS = (4, 4, 4, 4)
+AHEAD = 1
 PLACES = 9
+UNROLL = 8
 VMEM_BYTES = 60 * 1024 * 1024
 
 
@@ -33,17 +35,18 @@
     y_up, y_down = lax.rem(y + 1, 4), lax.rem(y + 3, 4)
     x_up, x_down = lax.rem(i + 2, n_dom), lax.rem(i + n_dom - 2, n_dom)
     partner = i + 1 - 2 * core
-    rows = h_ref.shape[0] // NC
-    half = rows // 2
-    blocks = rows // PACK
+    NC = len(CHUNKS)
+    first_row = [sum(CHUNKS[:n]) * PACK for n in range(NC)]
 
     def hrows(n, part=None):
+        size = CHUNKS[n] * PACK
         if part is None:
-            return pl.ds(n * rows, rows)
-        return pl.ds(n * rows + part * half, half)
+            return pl.ds(first_row[n], size)
+        return pl.ds(first_row[n] + part * (size // 2), size // 2)
 
     def grows(n):
-        return pl.ds(0, HEAD + rows) if n == 0 else pl.ds(HEAD + n * rows, rows)
+        size = CHUNKS[n] * PACK
+        return pl.ds(0, HEAD + size) if n == 0 else pl.ds(HEAD + first_row[n], size)
 
     def remote(src, dst, send, recv, dom, feat):
         return pltpu.make_async_remote_copy(
@@ -63,7 +66,8 @@
 
     sent = []
     up, down = [], []
-    for n in range(NC):
+
+    def gather_own(n):
         loads[n].wait()
         a = remote(held.at[y, hrows(n)], held.at[y, hrows(n)], ysend.at[0, n], yrecv.at[0, n], i, y_up)
         b = remote(held.at[y, hrows(n)], held.at[y, hrows(n)], ysend.at[1, n], yrecv.at[1, n], i, y_down)
@@ -71,7 +75,10 @@
         b.start()
         up.append(a)
         down.append(b)
-        sent += [a, b]
+        sent.extend([a, b])
+
+    for n in range(min(AHEAD, NC)):
+        gather_own(n)
 
     def gather_relay(n):
         up[n].wait_recv()
@@ -81,14 +88,17 @@
         b = remote(held.at[y_up, hrows(n, 1)], held.at[y_up, hrows(n, 1)], ysend.at[3, n], yrecv.at[3, n], i, y_down)
         b.start()
         sent.extend([a, b])
+        if n + AHEAD < NC:
+            gather_own(n + AHEAD)
         return a, b
 
     lane = lax.broadcasted_iota(jnp.int32, (64, LANES), 1)
     low = lane < 64
 
     def project(n):
+        blocks = CHUNKS[n]
         for j in range(blocks):
-            base = n * rows + j * PACK
+            base = first_row[n] + j * PACK
             out = slice(j * BLK, (j + 1) * BLK)
             top = slice(j * BLK, j * BLK + 64)
             bot = slice(j * BLK + 64, (j + 1) * BLK)
@@ -100,10 +110,10 @@
                 cols = slice(512 + pair * LANES, 512 + (pair + 1) * LANES)
                 lhs[top, cols] = jnp.concatenate([p0[:, :64], p1[:, :64]], axis=1)
                 lhs[bot, cols] = jnp.concatenate([p0[:, 64:], p1[:, 64:]], axis=1)
-        res = jnp.dot(lhs[...], w_ref[...], preferred_element_type=jnp.float32) + b_ref[...]
+        res = jnp.dot(lhs[:blocks * BLK], w_ref[...], preferred_element_type=jnp.float32) + b_ref[...]
         for j in range(blocks):
             r0 = j * BLK
-            base = n * rows + j * PACK
+            base = first_row[n] + j * PACK
             own[HEAD + base:HEAD + base + BLK, :] = res[r0:r0 + BLK, :LANES].astype(jnp.bfloat16)
             s_ref[base:base + BLK, :] = res[r0:r0 + BLK, LANES:2 * LANES]
             top = res[r0:r0 + 64, 2 * LANES:]
@@ -174,7 +184,7 @@
         copy.wait_send()
 
 
-def aggregate(last, tidx, roff, starts, g_ref, t_ref, s_ref, out_ref, gv, tv, g_sem, t_sem):
+def aggregate(last, tidx, roff, keep, ends, g_ref, t_ref, s_ref, out_ref, gv, tv, part, g_sem, t_sem):
     slot_rows = g_ref.shape[1]
     tiles = t_ref.shape[0]
     groups = 4
@@ -206,32 +216,40 @@
         ], axis=0)
         return jnp.concatenate([left, right], axis=1)
 
-    def block(b, carry):
-        def pair(p, acc):
-            q = 2 * p
-            lhs = jnp.concatenate([tv[tidx[q]], tv[tidx[q + 1]]], axis=1)
-            rhs = jnp.concatenate([source(q), source(q + 1)], axis=0)
-            return acc + jnp.dot(lhs, rhs, preferred_element_type=jnp.float32)
-
-        acc = lax.fori_loop(starts[b], starts[b + 1], pair, jnp.zeros((BLK, 2 * LANES), jnp.float32))
+    def product(p):
+        q = 2 * p
+        lhs = jnp.concatenate([tv[tidx[q]], tv[tidx[q + 1]]], axis=1)
+        rhs = jnp.concatenate([source(q), source(q + 1)], axis=0)
+        return jnp.dot(lhs, rhs, preferred_element_type=jnp.float32)
+
+    part[0] = jnp.zeros(part.shape[1:], jnp.float32)
+
+    def step(g, carry):
+        products = [product(g * UNROLL + u) for u in range(UNROLL)]
+        for u in range(UNROLL):
+            p = g * UNROLL + u
+            part[p + 1] = part[p] * keep[p] + products[u]
+        return carry
+
+    lax.fori_loop(0, (part.shape[0] - 1) // UNROLL, step, 0)
+
+    for b in range(s_ref.shape[0] // PACK):
+        acc = part[ends[b]]
         scale = 1.0 / (1.0 + acc[:, PACK:PACK + 1])
         left = acc[:, :LANES] * scale
         right = acc[:, LANES:] * scale
         pack = jnp.where(low, right[:64], pltpu.roll(right[64:], 64, 1))
-        base = pl.multiple_of(b * PACK, PACK)
-        left = left + s_ref[pl.ds(base, BLK), :]
-        pack = pack + s_ref[pl.ds(base + BLK, 64), :]
+        base = b * PACK
+        left = left + s_ref[base:base + BLK, :]
+        pack = pack + s_ref[base + BLK:base + PACK, :]
         if last:
-            row = pl.multiple_of(b * BLK, BLK)
-            out_ref[pl.ds(row, BLK), :LANES] = left.astype(jnp.bfloat16)
-            out_ref[pl.ds(row, 64), LANES:] = pack[:, :64].astype(jnp.bfloat16)
-            out_ref[pl.ds(row + 64, 64), LANES:] = pltpu.roll(pack, 64, 1)[:, :64].astype(jnp.bfloat16)
+            row = b * BLK
+            out_ref[row:row + BLK, :LANES] = left.astype(jnp.bfloat16)
+            out_ref[row:row + 64, LANES:] = pack[:, :64].astype(jnp.bfloat16)
+            out_ref[row + 64:row + BLK, LANES:] = pltpu.roll(pack, 64, 1)[:, :64].astype(jnp.bfloat16)
         else:
-            out_ref[pl.ds(base, BLK), :] = jnp.maximum(left, 0.0).astype(jnp.bfloat16)
-            out_ref[pl.ds(base + BLK, 64), :] = jnp.maximum(pack, 0.0).astype(jnp.bfloat16)
-        return carry
-
-    lax.fori_loop(0, s_ref.shape[0] // PACK, block, 0)
+            out_ref[base:base + BLK, :] = jnp.maximum(left, 0.0).astype(jnp.bfloat16)
+            out_ref[base + BLK:base + PACK, :] = jnp.maximum(pack, 0.0).astype(jnp.bfloat16)
 
 
 def per_device(
@@ -284,7 +302,12 @@
     here = place[None, :] == jnp.arange(entries, dtype=i32)[:, None]
     tidx = jnp.sum(jnp.where(here, ids[None, :] - tiles, 0), axis=1) + tiles
     sidx = jnp.sum(jnp.where(here, tile_src[None, :] + 1, 0), axis=1) - 1
-
+    steps = jnp.arange(entries // 2, dtype=i32)
+    opens = (steps[:, None] == starts[None, :blk_dev]) & (pairs[None, :] > 0)
+    keep = 1.0 - jnp.max(opens.astype(jnp.float32), axis=1)
+    ends = jnp.where(pairs > 0, starts[1:], 0)
+
+    NC = len(CHUNKS)
     exchange_call = pl.pallas_call(
         exchange,
         out_shape=(
@@ -301,7 +324,7 @@
         scratch_shapes=[
             pltpu.VMEM((4, packed_rows, LANES), jnp.bfloat16),
             pltpu.VMEM((slot_rows, LANES), jnp.bfloat16),
-            pltpu.VMEM((node_rows // NC, 768), jnp.bfloat16),
+            pltpu.VMEM((max(CHUNKS) * BLK, 768), jnp.bfloat16),
             pltpu.SemaphoreType.DMA((NC,)),
             pltpu.SemaphoreType.DMA((NC,)),
             pltpu.SemaphoreType.DMA,
@@ -324,7 +347,7 @@
             functools.partial(aggregate, last),
             out_shape=jax.ShapeDtypeStruct(out, jnp.bfloat16),
             grid_spec=pltpu.PrefetchScalarGridSpec(
-                num_scalar_prefetch=3,
+                num_scalar_prefetch=4,
                 grid=(),
                 in_specs=[
                     pl.BlockSpec(memory_space=pl.ANY),
@@ -335,6 +358,7 @@
                 scratch_shapes=[
                     pltpu.VMEM((zero_row + PACK, LANES), jnp.bfloat16),
                     pltpu.VMEM((tiles + 1, BLK, BLK), jnp.bfloat16),
+                    pltpu.VMEM((entries // 2 + 1, BLK, 2 * LANES), jnp.float32),
                     pltpu.SemaphoreType.DMA((PLACES,)),
                     pltpu.SemaphoreType.DMA((4,)),
                 ],
@@ -357,7 +381,7 @@
             rows = jnp.concatenate([mine, theirs])
             srcs = jnp.arange(rows.shape[0], dtype=i32)
             roff = jnp.sum(jnp.where(sidx[:, None] == srcs[None, :], rows[None, :] - zero_row, 0), axis=1) + zero_row
-        hidden = aggregate_call(layer == LAYERS - 1)(tidx, roff, starts, g, tile_vals, s)
+        hidden = aggregate_call(layer == LAYERS - 1)(tidx, roff, keep, ends, g, tile_vals, s)
     return hidden
 
 

time: 318 us -> 244 us (0.77)
  Pallas kernels: 294 us -> 221 us
    pallas_call x3, Pallas kernels: 96.1 us -> 43.3 us  [per_device(): aggregate_call(layer == LAYERS - 1)(tidx, roff, keep, ends, g, tile_vals, s)]
    pallas_call x3, Pallas kernels: 198 us -> 178 us  [per_device(): g, s = exchange_call(hidden, table, w[layer], b_all[layer])]
where the time goes in v2:
time: 244 us; the launch traced here: 242 us
  Pallas kernels  221 us (91%)
  other arithmetic  10.2 us (4%)
  local copies, waits for them, and re-layouts  10 us (4%)
    pallas_call x3, Pallas kernels, per_device(): g, s = exchange_call(hidden, table, w[layer], b_all[layer])  178 us
    pallas_call x3, Pallas kernels, per_device(): aggregate_call(layer == LAYERS - 1)(tidx, roff, keep, ends, g, tile_vals, s)  43.3 us

profile of v2, /device:TPU:0, one launch (start us, length us, event | category | flops | bytes accessed | tf_op | source)
XLA Modules:
  0.0 242.2 jit_solution(7605834173259480166)
XLA Ops:
  0.0 3.2 %constant_dynamic-slice_fusion.1 = (bf16[3,768,192]{2,1,0:T(8,128)(2,1)S(1)}, bf16[3,768,192]{2,1,0:T(8,128)(2,1)S(1)}) fusion(bf16[3,768,768]{2,1,0:T(8,128)(2,1)} %param.23, s32[]{:T(128)S(6)} %select_n.57, bf16[3,768,768]{2,1,0:T(8,128)(2,1)} %param.24), kind=kLoop, calls=%fused_computation.48 | loop fusion | bytes 3538948 | tf_op jit(solution)/shard_map/dynamic_slice | solution.py:269
  3.2 0.1 slice.138
  3.3 0.1 slice.139
  3.4 0.1 slice.140
  3.6 0.1 slice.141
  3.7 0.5 pad_maximum_fusion
  4.2 0.1 slice.142
  4.3 0.2 pad_maximum_fusion.2
  4.5 0.0 copy-start.9
  4.5 1.4 fusion.4
  5.9 0.1 constant_dynamic-slice_fusion
  5.9 0.1 constant_dynamic-slice_fusion.3
  6.0 0.1 pad_maximum_fusion.3
  6.1 0.6 fusion.10
  6.7 0.6 fusion.11
  7.3 0.1 copy.26
  7.4 0.7 and_reduce_fusion
  8.1 2.1 dynamic-slice_select_fusion
  10.2 1.6 scatter.9.tab_ref
  11.9 0.5 copy.28
  12.4 0.1 fusion.9
  12.5 0.1 slice.135
  12.6 0.0 copy-start.7
  12.6 0.0 copy-start.6
  12.7 1.1 maximum_maximum_fusion
  13.7 59.5 %exchange.3 = (bf16[9,3088,128]{2,1,0:T(8,128)(2,1)}, f32[3072,128]{1,0:T(8,128)}) custom-call(bf16[3072,128]{1,0:T(8,128)(2,1)} %bitcast.28, bf16[16,128]{1,0:T(8,128)(2,1)} %copy-done.2, bf16[768,384]{1,0:T(8,128)(2,1)} %get-tuple-element.46.w_ref, f32[1,384]{1,0:T(1,128)} %get-tuple-element.52.b_ref), custom_call_target="tpu_custom_call" | custom-call | tf_op jit(solution)/shard_map/exchange/pallas_call | solution.py:372
  73.3 0.8 multiply_reduce_fusion
  74.1 0.2 slice_reduce_fusion
  74.3 0.1 add_select_fusion
  74.3 0.1 concatenate.33
  74.4 0.1 add_add_fusion
  75.2 0.1 convert_reduce_fusion.1
  75.3 0.1 select_reduce_fusion.3
  75.4 0.2 convert_reduce_fusion
  75.6 0.2 select_reduce_fusion
  75.8 0.6 broadcast_add_fusion.1
  76.4 0.1 select_reduce_fusion.2
  76.5 0.6 broadcast_add_fusion.roff
  77.1 0.1 select_reduce_fusion.4
  77.2 0.7 slice_select_fusion
  77.8 0.1 convert_reduce_fusion.2
  77.9 0.6 broadcast_subtract_fusion.keep
  78.5 14.1 %aggregate.2.h_ref = bf16[3072,128]{1,0:T(8,128)(2,1)} custom-call(s32[208]{0:T(256)} %get-tuple-element.58.tidx, s32[208]{0:T(256)} %broadcast_add_fusion.roff, f32[104]{0:T(128)} %broadcast_subtract_fusion.keep, s32[16]{0:T(128)} %get-tuple-element.53.ends, bf16[9,3088,128]{2,1,0:T(8,128)(2,1)} %get-tuple-element.35.g_ref, bf16[192,128,128]{2,1,0:T(8,128)(2,1)} %t_ref.5, ...), custom_call_target="tpu_custom_call" | custom-call | tf_op jit(solution)/shard_map/aggregate/pallas_call | solution.py:384
  92.6 59.3 %exchange.4 = (bf16[9,3088,128]{2,1,0:T(8,128)(2,1)}, f32[3072,128]{1,0:T(8,128)}) custom-call(bf16[3072,128]{1,0:T(8,128)(2,1)} %aggregate.2.h_ref, bf16[16,128]{1,0:T(8,128)(2,1)} %copy-done.2, bf16[768,384]{1,0:T(8,128)(2,1)} %get-tuple-element.47.w_ref, f32[1,384]{1,0:T(1,128)} %get-tuple-element.51.b_ref), custom_call_target="tpu_custom_call" | custom-call | tf_op jit(solution)/shard_map/exchange/pallas_call | solution.py:372
  151.9 14.3 %aggregate.3.h_ref = bf16[3072,128]{1,0:T(8,128)(2,1)} custom-call(s32[208]{0:T(256)} %get-tuple-element.58.tidx, s32[208]{0:T(256)} %broadcast_add_fusion.roff, f32[104]{0:T(128)} %broadcast_subtract_fusion.keep, s32[16]{0:T(128)} %get-tuple-element.53.ends, bf16[9,3088,128]{2,1,0:T(8,128)(2,1)} %get-tuple-element.37.g_ref, bf16[192,128,128]{2,1,0:T(8,128)(2,1)} %t_ref.5, ...), custom_call_target="tpu_custom_call" | custom-call | tf_op jit(solution)/shard_map/aggregate/pallas_call | solution.py:384
  166.1 58.8 %exchange.5 = (bf16[9,3088,128]{2,1,0:T(8,128)(2,1)}, f32[3072,128]{1,0:T(8,128)}) custom-call(bf16[3072,128]{1,0:T(8,128)(2,1)} %aggregate.3.h_ref, bf16[16,128]{1,0:T(8,128)(2,1)} %copy-done.2, bf16[768,384]{1,0:T(8,128)(2,1)} %get-tuple-element.45.w_ref, f32[1,384]{1,0:T(1,128)} %get-tuple-element.50.b_ref), custom_call_target="tpu_custom_call" | custom-call | tf_op jit(solution)/shard_map/exchange/pallas_call | solution.py:372
  225.0 15.0 %aggregate_last.1 = bf16[2048,192]{1,0:T(8,128)(2,1)} custom-call(s32[208]{0:T(256)} %get-tuple-element.58.tidx, s32[208]{0:T(256)} %broadcast_add_fusion.roff, f32[104]{0:T(128)} %broadcast_subtract_fusion.keep, s32[16]{0:T(128)} %get-tuple-element.53.ends, bf16[9,3088,128]{2,1,0:T(8,128)(2,1)} %get-tuple-element.39.g_ref, bf16[192,128,128]{2,1,0:T(8,128)(2,1)} %t_ref.5, ...), custom_call_target="tpu_custom_call" | custom-call | tf_op jit(solution)/shard_map/aggregate_last/pallas_call | solution.py:384
  240.0 2.2 copy.27
  (33 shorter events, 0.1 us)
Async XLA Ops:
  0.0 5.8 %copy-start = (f32[3,768]{1,0:T(4,128)S(1)}, f32[3,768]{1,0:T(4,128)}, u32[]{:S(2)}) copy-start(f32[3,768]{1,0:T(4,128)} %param.25) | copy-start | bytes 27652
  4.4 2.9 %copy-start.4 = (s32[1,8,8]{2,1,0:T(8,128)S(1)}, s32[1,8,8]{2,1,0:T(8,128)}, u32[]{:S(2)}) copy-start(s32[1,8,8]{2,1,0:T(8,128)} %param.21) | copy-start | bytes 772
  4.4 2.8 %copy-start.8 = (s32[1,8]{1,0:T(1,128)S(1)}, s32[1,8]{1,0:T(1,128)}, u32[]{:S(2)}) copy-start(s32[1,8]{1,0:T(1,128)} %param.22) | copy-start | bytes 100
  4.5 2.9 %copy-start.9 = (s32[2]{0:T(128)S(1)}, s32[2]{0:T(128)}, u32[]{:S(2)}) copy-start(s32[2]{0:T(128)} %constant.99.clone.1) | copy-start | bytes 28
  4.5 7.4 %copy-start.1 = (bf16[2048,192]{0,1:T(8,128)(2,1)S(1)}, bf16[2048,192]{0,1:T(8,128)(2,1)}, u32[]{:S(2)}) copy-start(bf16[2048,192]{0,1:T(8,128)(2,1)} %param.16) | copy-start | bytes 2359300
  11.9 0.7 copy-start.2
  12.6 60.6 %copy-start.7 = (s32[8]{0:T(128)S(1)}, s32[8]{0:T(128)}, u32[]{:S(2)}) copy-start(s32[8]{0:T(128)} %constant.110.clone) | copy-start | bytes 100
  12.6 61.7 %copy-start.6 = (s32[8]{0:T(128)S(1)}, s32[8]{0:T(128)}, u32[]{:S(2)}) copy-start(s32[8]{0:T(128)} %constant.117) | copy-start | bytes 100
  12.6 62.6 %copy-start.3 = (s32[192]{0:T(256)S(1)}, s32[192]{0:T(256)}, u32[]{:S(2)}) copy-start(s32[192]{0:T(256)} %param.18) | copy-start | bytes 2308
  12.6 63.0 %copy-start.5 = (s32[192]{0:T(256)S(1)}, s32[192]{0:T(256)}, u32[]{:S(2)}) copy-start(s32[192]{0:T(256)} %param.19) | copy-start | bytes 2308

commit v3 on v2

v3 whole, which is shorter than its diff:
```python
import functools

import jax
import jax.numpy as jnp
from jax import lax
from jax.experimental import pallas as pl
from jax.experimental.pallas import tpu as pltpu
from jax.sharding import PartitionSpec as P

LAYERS = 3
BLK = 128
PEERS = 8
SLOTS = 8
MESH = pl.DeviceIdType.MESH
LANES = 128
PACK = 192
HEAD = 16
CHUNKS = (4, 4, 4, 4)
AHEAD = 1
PLACES = 9
UNROLL = 8
EXCHANGE_BYTES = 32 * 1024 * 1024
AGGREGATE_BYTES = 40 * 1024 * 1024


def offset(d):
    return (d // 2 + 1) * (1 if d % 2 == 0 else -1)


def cut(raw, odd):
    t0, t1 = raw[:, :128], raw[:, 128:]
    first = jnp.where(odd, jnp.concatenate([t0[:, 64:], t1[:, :64]], axis=1), t0)
    rest = jnp.where(odd, t1[:, 64:], t1[:, :64])
    return first, rest


def order_tiles(count, dst, src, g_ref, idx_ref):
    f32 = jnp.float32
    wide = 2 * LANES
    slot_rows = g_ref.shape[1]
    zero_row = PLACES * slot_rows
    tiles = dst.shape[1]
    pad = jnp.zeros((1, wide - tiles), f32)
    lane = lax.broadcasted_iota(jnp.int32, (1, wide), 1)
    live = lane < count
    dst = jnp.where(live, jnp.concatenate([dst.astype(f32), pad], axis=1), float(wide))
    src = jnp.concatenate([src.astype(f32), pad], axis=1)
    square = (wide, wide)
    row_id = lax.broadcasted_iota(jnp.int32, square, 0).astype(f32)
    col_id = lax.broadcasted_iota(jnp.int32, square, 1).astype(f32)
    dst_row = jnp.broadcast_to(dst, square)
    dst_col = jnp.transpose(dst_row)
    src_col = jnp.transpose(jnp.broadcast_to(src, square))
    rank = jnp.sum(jnp.where((dst_row == dst_col) & (row_id < col_id), 1.0, 0.0), axis=0, keepdims=True)
    many_col = jnp.sum(jnp.where(dst_row == row_id, 1.0, 0.0)[:16], axis=1, keepdims=True)
    many_row = jnp.sum(jnp.where(dst_col == col_id, 1.0, 0.0), axis=0, keepdims=True)
    pairs_col = jnp.floor((many_col + 1.0) * 0.5)
    pairs_row = jnp.where(lane < 16, jnp.floor((many_row + 1.0) * 0.5), 0.0)
    few_row, few_col = row_id[:16], col_id[:16]
    start_col = jnp.sum(jnp.where(few_col < few_row, pairs_row, 0.0), axis=1, keepdims=True)
    before = jnp.sum(jnp.where(few_row < dst, pairs_col, 0.0), axis=0, keepdims=True)
    place = jnp.where(live, 2.0 * before + rank, -1.0)
    hit = jnp.where(jnp.transpose(jnp.broadcast_to(place, square)) == col_id, 1.0, 0.0)
    offs = jnp.where(lane < 16, 4.0 * slot_rows + HEAD + PACK * lane.astype(f32), 0.0)[:, :LANES]
    short = lane[:, :LANES]
    for d in range(PEERS):
        spot = 4 - offset(d)
        table = g_ref[spot, :HEAD, :].astype(f32)[d:d + 1]
        first = jnp.where(short.astype(f32) < table[:, SLOTS:SLOTS + 1], float(spot * slot_rows + HEAD) + PACK * table,
                          float(zero_row))
        first = jnp.where(short < SLOTS, first, 0.0)
        offs = offs + pltpu.roll(jnp.broadcast_to(first, (8, LANES)), 16 + SLOTS * d, 1)[:1]
    offs = jnp.concatenate([offs, jnp.zeros((1, LANES), f32)], axis=1)
    from_col = jnp.sum(jnp.where(src_col == col_id, offs, 0.0), axis=1, keepdims=True)
    opens = jnp.sum(jnp.where((start_col == few_col) & (pairs_col > 0.0), 1.0, 0.0), axis=0, keepdims=True)
    ends = jnp.sum(jnp.where(few_row <= few_col, pairs_col, 0.0), axis=0, keepdims=True)
    rows = (
        jnp.sum(hit * row_id, axis=0, keepdims=True),
        jnp.sum(hit * (from_col - zero_row), axis=0, keepdims=True) + zero_row,
        jnp.sum(hit, axis=0, keepdims=True),
        1.0 - opens,
        jnp.where(pairs_row > 0.0, ends, 0.0),
    )
    for k, row in enumerate(rows):
        idx_ref[k:k + 1, :] = row.astype(jnp.int32)


def exchange(layer, count_ref, h_ref, tab_ref, ws_ref, wn_ref, b_ref, dst_ref, src_ref, g_ref, s_ref, idx_ref,
             held, lhs, raw, w_ref, load_sem, tab_sem, raw_sem, ysend, yrecv, xsend, xrecv, psend, precv):
    i = lax.axis_index("dom")
    y = lax.axis_index("feat")
    n_dom = lax.axis_size("dom")
    core = lax.rem(i, 2)
    y_up, y_down = lax.rem(y + 1, 4), lax.rem(y + 3, 4)
    x_up, x_down = lax.rem(i + 2, n_dom), lax.rem(i + n_dom - 2, n_dom)
    partner = i + 1 - 2 * core
    NC = len(CHUNKS)
    first_row = [sum(CHUNKS[:n]) * PACK for n in range(NC)]

    def hrows(n, part=None):
        size = CHUNKS[n] * PACK
        if part is None:
            return pl.ds(first_row[n], size)
        return pl.ds(first_row[n] + part * (size // 2), size // 2)

    def grows(n):
        size = CHUNKS[n] * PACK
        return pl.ds(0, HEAD + size) if n == 0 else pl.ds(HEAD + first_row[n], size)

    def remote(src, dst, send, recv, dom, feat):
        return pltpu.make_async_remote_copy(
            src_ref=src, dst_ref=dst, send_sem=send, recv_sem=recv,
            device_id=(dom, feat), device_id_type=MESH)

    loads = [pltpu.make_async_copy(h_ref.at[hrows(n)], held.at[y, hrows(n)], load_sem.at[n]) for n in range(NC)]
    for load in loads:
        load.start()
    tab_load = pltpu.make_async_copy(tab_ref, g_ref.at[4, pl.ds(0, HEAD)], tab_sem)
    tab_load.start()
    window = pl.ds(pl.multiple_of((3 * y // 2) * LANES, LANES), 2 * LANES)
    raws = [pltpu.make_async_copy(ref.at[layer, :, window], raw.at[k], raw_sem.at[k]) for k, ref in enumerate((wn_ref, ws_ref))]
    for load in raws:
        load.start()

    barrier = pltpu.get_barrier_semaphore()
    for dom, feat in ((i, y_up), (i, y_down), (x_up, y), (x_down, y), (partner, y)):
        pl.semaphore_signal(barrier, inc=1, device_id=(dom, feat), device_id_type=MESH)
    pl.semaphore_wait(barrier, 5)

    sent = []
    up, down = [], []

    def gather_own(n):
        loads[n].wait()
        a = remote(held.at[y, hrows(n)], held.at[y, hrows(n)], ysend.at[0, n], yrecv.at[0, n], i, y_up)
        b = remote(held.at[y, hrows(n)], held.at[y, hrows(n)], ysend.at[1, n], yrecv.at[1, n], i, y_down)
        a.start()
        b.start()
        up.append(a)
        down.append(b)
        sent.extend([a, b])

    for n in range(min(AHEAD, NC)):
        gather_own(n)

    def gather_relay(n):
        up[n].wait_recv()
        a = remote(held.at[y_down, hrows(n, 0)], held.at[y_down, hrows(n, 0)], ysend.at[2, n], yrecv.at[2, n], i, y_up)
        a.start()
        down[n].wait_recv()
        b = remote(held.at[y_up, hrows(n, 1)], held.at[y_up, hrows(n, 1)], ysend.at[3, n], yrecv.at[3, n], i, y_down)
        b.start()
        sent.extend([a, b])
        if n + AHEAD < NC:
            gather_own(n + AHEAD)
        return a, b

    lane = lax.broadcasted_iota(jnp.int32, (64, LANES), 1)
    low = lane < 64

    def project(n):
        blocks = CHUNKS[n]
        for j in range(blocks):
            base = first_row[n] + j * PACK
            out = slice(j * BLK, (j + 1) * BLK)
            top = slice(j * BLK, j * BLK + 64)
            bot = slice(j * BLK + 64, (j + 1) * BLK)
            for a in range(4):
                lhs[out, a * LANES:(a + 1) * LANES] = held[a, base:base + BLK, :]
            for pair in range(2):
                p0 = held[2 * pair, base + BLK:base + PACK, :]
                p1 = held[2 * pair + 1, base + BLK:base + PACK, :]
                cols = slice(512 + pair * LANES, 512 + (pair + 1) * LANES)
                lhs[top, cols] = jnp.concatenate([p0[:, :64], p1[:, :64]], axis=1)
                lhs[bot, cols] = jnp.concatenate([p0[:, 64:], p1[:, 64:]], axis=1)
        res = jnp.dot(lhs[:blocks * BLK], w_ref[...], preferred_element_type=jnp.float32) + bias
        for j in range(blocks):
            r0 = j * BLK
            base = first_row[n] + j * PACK
            g_ref[4, HEAD + base:HEAD + base + BLK, :] = res[r0:r0 + BLK, :LANES].astype(jnp.bfloat16)
            s_ref[base:base + BLK, :] = res[r0:r0 + BLK, LANES:2 * LANES]
            top = res[r0:r0 + 64, 2 * LANES:]
            bot = res[r0 + 64:r0 + BLK, 2 * LANES:]
            g_ref[4, HEAD + base + BLK:HEAD + base + PACK, :] = jnp.where(
                low, top, pltpu.roll(bot, 64, 1)).astype(jnp.bfloat16)
            s_ref[base + BLK:base + PACK, :] = jnp.where(low, pltpu.roll(top, 64, 1), bot)

    ours, first, second = [], [], []

    def send_own(n):
        src = g_ref.at[4, grows(n)]
        a = remote(src, g_ref.at[2, grows(n)], xsend.at[0, n], xrecv.at[0, n], x_up, y)
        b = remote(src, g_ref.at[6, grows(n)], xsend.at[1, n], xrecv.at[1, n], x_down, y)
        c = remote(src, g_ref.at[3 + 2 * core, grows(n)], psend.at[0, n], precv.at[0, n], partner, y)
        for copy in (a, b, c):
            copy.start()
        ours.append((a, b, c))
        sent.extend([a, b, c])

    def relay_one(n):
        a, b, _ = ours[n]
        a.wait_recv()
        u = remote(g_ref.at[2, grows(n)], g_ref.at[0, grows(n)], xsend.at[2, n], xrecv.at[2, n], x_up, y)
        pu = remote(g_ref.at[2, grows(n)], g_ref.at[1 + 2 * core, grows(n)], psend.at[1, n], precv.at[1, n], partner, y)
        u.start()
        pu.start()
        b.wait_recv()
        v = remote(g_ref.at[6, grows(n)], g_ref.at[8, grows(n)], xsend.at[3, n], xrecv.at[3, n], x_down, y)
        pv = remote(g_ref.at[6, grows(n)], g_ref.at[5 + 2 * core, grows(n)], psend.at[2, n], precv.at[2, n], partner, y)
        v.start()
        pv.start()
        first.append((u, v, pu, pv))
        sent.extend([u, v, pu, pv])

    def relay_two(n):
        u, v, _, _ = first[n]
        u.wait_recv()
        v.wait_recv()
        c = remote(g_ref.at[8 - 8 * core, grows(n)], g_ref.at[7 - 6 * core, grows(n)], psend.at[3, n], precv.at[3, n],
                   partner, y)
        c.start()
        second.append(c)
        sent.append(c)

    g_ref[PLACES, :PACK, :] = jnp.zeros((PACK, LANES), jnp.bfloat16)
    odd = lax.rem(y, 2) == 1
    for load in raws:
        load.wait()
    n_first, n_rest = cut(raw[0], odd)
    s_first, s_rest = cut(raw[1], odd)
    rest = jnp.concatenate([n_rest, s_rest], axis=1)
    for a in range(4):
        for part, cols in ((n_first, 0), (s_first, 1), (rest, 2)):
            cols = slice(cols * LANES, (cols + 1) * LANES)
            w_ref[a * BLK:(a + 1) * BLK, cols] = part[a * PACK:a * PACK + BLK]
            w_ref[512 + a * 64:512 + (a + 1) * 64, cols] = part[a * PACK + BLK:(a + 1) * PACK]
    b_first, b_rest = cut(b_ref[layer:layer + 1, window], odd)
    bias = jnp.concatenate([jnp.zeros((1, LANES), jnp.float32), b_first, jnp.zeros((1, 64), jnp.float32), b_rest], axis=1)

    tab_load.wait()
    for n in range(NC):
        a, b = gather_relay(n)
        a.wait_recv()
        b.wait_recv()
        project(n)
        send_own(n)
        if n >= 1:
            relay_one(n - 1)
        if n >= 2:
            relay_two(n - 2)
    relay_one(NC - 1)
    for n in range(1):
        ours[n][2].wait_recv()
        first[n][2].wait_recv()
        first[n][3].wait_recv()
        second[n].wait_recv()
    order_tiles(count_ref[0], dst_ref[...], src_ref[...], g_ref, idx_ref)
    for n in range(max(NC - 2, 0), NC):
        relay_two(n)
    for n in range(1, NC):
        ours[n][2].wait_recv()
        first[n][2].wait_recv()
        first[n][3].wait_recv()
        second[n].wait_recv()
    for copy in sent:
        copy.wait_send()


def aggregate(last, idx, gv, tv, s_ref, out_ref, part):
    lane = lax.broadcasted_iota(jnp.int32, (64, LANES), 1)
    low = lane < 64

    def source(q):
        row = pl.multiple_of(idx[1, q], 16)
        ones = jnp.full((64, 64), idx[2, q].astype(jnp.float32)).astype(jnp.bfloat16)
        left = gv[pl.ds(row, BLK), :]
        pack = gv[pl.ds(row + BLK, 64), :]
        right = jnp.concatenate([
            jnp.concatenate([pack[:, :64], ones], axis=1),
            jnp.concatenate([pack[:, 64:], ones], axis=1),
        ], axis=0)
        return jnp.concatenate([left, right], axis=1)

    def product(p):
        q = 2 * p
        lhs = jnp.concatenate([tv[idx[0, q]], tv[idx[0, q + 1]]], axis=1)
        rhs = jnp.concatenate([source(q), source(q + 1)], axis=0)
        return jnp.dot(lhs, rhs, preferred_element_type=jnp.float32)

    part[0] = jnp.zeros(part.shape[1:], jnp.float32)

    def step(g, carry):
        products = [product(g * UNROLL + u) for u in range(UNROLL)]
        for u in range(UNROLL):
            p = g * UNROLL + u
            part[p + 1] = part[p] * idx[3, p].astype(jnp.float32) + products[u]
        return carry

    lax.fori_loop(0, (part.shape[0] - 1) // UNROLL, step, 0)

    for b in range(s_ref.shape[0] // PACK):
        acc = part[idx[4, b]]
        scale = 1.0 / (1.0 + acc[:, PACK:PACK + 1])
        left = acc[:, :LANES] * scale
        right = acc[:, LANES:] * scale
        pack = jnp.where(low, right[:64], pltpu.roll(right[64:], 64, 1))
        base = b * PACK
        left = left + s_ref[base:base + BLK, :]
        pack = pack + s_ref[base + BLK:base + PACK, :]
        if last:
            row = b * BLK
            out_ref[row:row + BLK, :LANES] = left.astype(jnp.bfloat16)
            out_ref[row:row + 64, LANES:] = pack[:, :64].astype(jnp.bfloat16)
            out_ref[row + 64:row + BLK, LANES:] = pltpu.roll(pack, 64, 1)[:, :64].astype(jnp.bfloat16)
        else:
            out_ref[base:base + BLK, :] = jnp.maximum(left, 0.0).astype(jnp.bfloat16)
            out_ref[base + BLK:base + PACK, :] = jnp.maximum(pack, 0.0).astype(jnp.bfloat16)


def per_device(
    feats, tile_vals, tile_dst, tile_src, tile_count, send_blocks, send_count, w_self, w_nbr, bias
):
    node_rows, cols = feats.shape
    blk_dev = node_rows // BLK
    packed_rows = blk_dev * PACK
    slot_rows = HEAD + packed_rows
    tiles = tile_vals.shape[0]
    entries = tiles + blk_dev

    f3 = feats.reshape(blk_dev, BLK, cols)
    hidden = jnp.concatenate(
        [f3[..., :128], jnp.concatenate([f3[:, :64, 128:], f3[:, 64:, 128:]], axis=2)], axis=1
    ).reshape(packed_rows, LANES)

    table = jnp.concatenate([send_blocks[0], send_count[0][:, None]], axis=1).astype(jnp.bfloat16)
    table = jnp.pad(table, ((0, HEAD - PEERS), (0, LANES - SLOTS - 1)))

    NC = len(CHUNKS)
    vmem = pl.BlockSpec(memory_space=pltpu.VMEM)
    hbm = pl.BlockSpec(memory_space=pl.ANY)

    def exchange_call(layer):
        return pl.pallas_call(
            functools.partial(exchange, layer),
            out_shape=(
                jax.ShapeDtypeStruct((PLACES + 1, slot_rows, LANES), jnp.bfloat16),
                jax.ShapeDtypeStruct((packed_rows, LANES), jnp.float32),
                jax.ShapeDtypeStruct((8, 2 * LANES), jnp.int32),
            ),
            in_specs=[pl.BlockSpec(memory_space=pltpu.SMEM), hbm, hbm, hbm, hbm, vmem, vmem, vmem],
            out_specs=(vmem, vmem, vmem),
            scratch_shapes=[
                pltpu.VMEM((4, packed_rows, LANES), jnp.bfloat16),
                pltpu.VMEM((max(CHUNKS) * BLK, 768), jnp.bfloat16),
                pltpu.VMEM((2, 768, 2 * LANES), jnp.bfloat16),
                pltpu.VMEM((768, 3 * LANES), jnp.bfloat16),
                pltpu.SemaphoreType.DMA((NC,)),
                pltpu.SemaphoreType.DMA,
                pltpu.SemaphoreType.DMA((2,)),
            ] + [pltpu.SemaphoreType.DMA((4, NC)) for _ in range(6)],
            compiler_params=pltpu.CompilerParams(
                collective_id=layer, has_side_effects=True, vmem_limit_bytes=EXCHANGE_BYTES
            ),
            name=f"exchange{layer}",
        )

    def aggregate_call(last):
        out = (node_rows, cols) if last else (packed_rows, LANES)
        return pl.pallas_call(
            functools.partial(aggregate, last),
            out_shape=jax.ShapeDtypeStruct(out, jnp.bfloat16),
            grid_spec=pltpu.PrefetchScalarGridSpec(
                num_scalar_prefetch=1,
                grid=(),
                in_specs=[vmem, vmem, vmem],
                out_specs=vmem,
                scratch_shapes=[pltpu.VMEM((entries // 2 + 1, BLK, 2 * LANES), jnp.float32)],
            ),
            compiler_params=pltpu.CompilerParams(vmem_limit_bytes=AGGREGATE_BYTES),
            name="aggregate_last" if last else "aggregate",
        )

    dsts, srcs = tile_dst[None, :], tile_src[None, :]
    for layer in range(LAYERS):
        g, s, idx = exchange_call(layer)(tile_count, hidden, table, w_self, w_nbr, bias, dsts, srcs)
        g = g.reshape((PLACES + 1) * slot_rows, LANES)
        hidden = aggregate_call(layer == LAYERS - 1)(idx, g, tile_vals, s)
    return hidden


def solution(mesh):
    in_specs = (
        P("dom", "feat"),
        P("dom", None, None),
        P("dom"),
        P("dom"),
        P("dom"),
        P("dom", None, None),
        P("dom", None),
        P(),
        P(),
        P(),
    )
    out_specs = P("dom", "feat")
    return jax.shard_map(
        per_device, mesh=mesh, in_specs=in_specs, out_specs=out_specs, check_vma=False
    )
```

time: 244 us -> 224 us (0.918)
  Pallas kernels: 221 us -> 204 us
  other arithmetic: 10.2 us -> 1.62 us
  local copies, waits for them, and re-layouts: 10 us -> 16 us
    pallas_call x6, Pallas kernels: 221 us -> 204 us  [the longest x3 172 us: per_device(): exchange_call(layer)]
    unnamed x20 -> x22, local copies, waits for them, and re-layouts: 0.06 us -> 13 us
    dynamic_slice x1 -> x0, local copies, waits for them, and re-layouts: 3.21 us -> none  [cut(): here = lax.dynamic_slice_in_dim(w, y * cols, cols, 2)]
where the time goes in v3:
time: 224 us; the launch traced here: 222 us
  Pallas kernels  204 us (91%)
  local copies, waits for them, and re-layouts  16 us (7%)
    pallas_call x3, Pallas kernels, per_device(): exchange_call(layer)  172 us
    pallas_call x3, Pallas kernels, per_device(): hidden = aggregate_call(layer == LAYERS - 1)(idx, g, tile_vals, s)  31.5 us
    unnamed x22, local copies, waits for them, and re-layouts  13 us

profile of v3, /device:TPU:0, one launch (start us, length us, event | category | flops | bytes accessed | tf_op | source)
XLA Modules:
  0.0 222.0 jit_solution(1634039952615068053)
XLA Ops:
  0.7 0.7 convert_bitcast_fusion.1
  1.3 0.1 copy.14
  1.4 0.7 convert_bitcast_fusion
  2.1 0.1 fusion.5.tab_ref
  2.2 0.0 copy-start.6
  2.2 0.0 copy-start.7
  2.2 0.0 copy-start.8
  2.2 1.5 copy.16
  3.7 0.0 copy-start
  3.7 0.0 slice-start
  3.7 0.1 slice.12
  3.8 0.1 fusion.6
  3.9 0.2 maximum_maximum_fusion
  4.1 0.0 copy-done.6
  4.1 0.0 copy-done.7
  4.1 0.0 copy-done.8
  4.1 1.5 copy-done
  5.7 0.0 copy-start.1
  5.7 2.3 %copy-done.1 = bf16[3,768,768]{2,1,0:T(8,128)(2,1)S(1)} copy-done((bf16[3,768,768]{2,1,0:T(8,128)(2,1)S(1)}, bf16[3,768,768]{2,1,0:T(8,128)(2,1)}, u32[]{:S(2)}) %copy-start.1) | copy-done | bytes 3538968
  7.9 0.0 slice-start.1
  7.9 58.0 %exchange0.1 = (bf16[10,3088,128]{2,1,0:T(8,128)(2,1)S(1)}, f32[3072,128]{1,0:T(8,128)S(1)}, s32[8,256]{1,0:T(8,128)S(1)}) custom-call(s32[1]{0:T(128)S(6)} %copy.17.count_ref, bf16[3072,128]{1,0:T(8,128)(2,1)S(1)} %bitcast.16, bf16[16,128]{1,0:T(8,128)(2,1)S(1)} %fusion.5.tab_ref, bf16[3,768,768]{2,1,0:T(8,128)(2,1)S(1)} %copy-done, ...), custom_call_target="tpu_custom_call" | custom-call | tf_op jit(solution)/shard_map/exchange0/pallas_call | solution.py:385
  65.9 0.0 copy-start.4
  65.9 3.1 %copy-done.4 = bf16[10,3088,128]{2,1,0:T(8,128)(2,1)} copy-done((bf16[10,3088,128]{2,1,0:T(8,128)(2,1)}, bf16[10,3088,128]{2,1,0:T(8,128)(2,1)S(1)}, u32[]{:S(2)}) %copy-start.4) | copy-done | bytes 7905304
  69.0 0.0 slice-done
  69.0 0.0 slice-done.1
  69.0 0.0 copy-start.2
  69.0 10.4 %aggregate.2.h_ref = bf16[3072,128]{1,0:T(8,128)(2,1)S(1)} custom-call(s32[8,256]{1,0:T(8,128)S(1)} %get-tuple-element.14.idx, bf16[30880,128]{1,0:T(8,128)(2,1)} %bitcast.14, bf16[192,128,128]{2,1,0:T(8,128)(2,1)S(1)} %bitcast.12, f32[3072,128]{1,0:T(8,128)S(1)} %get-tuple-element.16.s_ref), custom_call_target="tpu_custom_call" | custom-call | tf_op jit(solution)/shard_map/aggregate/pallas_call | solution.py:387
  79.4 0.0 copy-done.2
  79.4 56.8 %exchange1.1 = (bf16[10,3088,128]{2,1,0:T(8,128)(2,1)S(1)}, f32[3072,128]{1,0:T(8,128)S(1)}, s32[8,256]{1,0:T(8,128)S(1)}) custom-call(s32[1]{0:T(128)S(6)} %copy.17.count_ref, bf16[3072,128]{1,0:T(8,128)(2,1)S(1)} %aggregate.2.h_ref, bf16[16,128]{1,0:T(8,128)(2,1)S(1)} %fusion.5.tab_ref, bf16[3,768,768]{2,1,0:T(8,128)(2,1)S(1)} %copy-done, ...), custom_call_target="tpu_custom_call" | custom-call | tf_op jit(solution)/shard_map/exchange1/pallas_call | solution.py:385
  136.3 0.0 copy-start.5
  136.3 3.1 %copy-done.5 = bf16[10,3088,128]{2,1,0:T(8,128)(2,1)} copy-done((bf16[10,3088,128]{2,1,0:T(8,128)(2,1)}, bf16[10,3088,128]{2,1,0:T(8,128)(2,1)S(1)}, u32[]{:S(2)}) %copy-start.5) | copy-done | bytes 7905304
  139.3 10.1 %aggregate.3.h_ref = bf16[3072,128]{1,0:T(8,128)(2,1)S(1)} custom-call(s32[8,256]{1,0:T(8,128)S(1)} %get-tuple-element.17.idx, bf16[30880,128]{1,0:T(8,128)(2,1)} %bitcast.15, bf16[192,128,128]{2,1,0:T(8,128)(2,1)S(1)} %bitcast.12, f32[3072,128]{1,0:T(8,128)S(1)} %get-tuple-element.19.s_ref), custom_call_target="tpu_custom_call" | custom-call | tf_op jit(solution)/shard_map/aggregate/pallas_call | solution.py:387
  149.5 57.3 %exchange2.1 = (bf16[10,3088,128]{2,1,0:T(8,128)(2,1)S(1)}, f32[3072,128]{1,0:T(8,128)S(1)}, s32[8,256]{1,0:T(8,128)S(1)}) custom-call(s32[1]{0:T(128)S(6)} %copy.17.count_ref, bf16[3072,128]{1,0:T(8,128)(2,1)S(1)} %aggregate.3.h_ref, bf16[16,128]{1,0:T(8,128)(2,1)S(1)} %fusion.5.tab_ref, bf16[3,768,768]{2,1,0:T(8,128)(2,1)S(1)} %copy-done, ...), custom_call_target="tpu_custom_call" | custom-call | tf_op jit(solution)/shard_map/exchange2/pallas_call | solution.py:385
  206.8 0.0 copy-start.3
  206.8 3.1 %copy-done.3 = bf16[10,3088,128]{2,1,0:T(8,128)(2,1)} copy-done((bf16[10,3088,128]{2,1,0:T(8,128)(2,1)}, bf16[10,3088,128]{2,1,0:T(8,128)(2,1)S(1)}, u32[]{:S(2)}) %copy-start.3) | copy-done | bytes 7905304
  209.9 10.9 %aggregate_last.1 = bf16[2048,192]{1,0:T(8,128)(2,1)S(1)} custom-call(s32[8,256]{1,0:T(8,128)S(1)} %get-tuple-element.20.idx, bf16[30880,128]{1,0:T(8,128)(2,1)} %bitcast.13, bf16[192,128,128]{2,1,0:T(8,128)(2,1)S(1)} %bitcast.12, f32[3072,128]{1,0:T(8,128)S(1)} %get-tuple-element.22.s_ref), custom_call_target="tpu_custom_call" | custom-call | tf_op jit(solution)/shard_map/aggregate_last/pallas_call | solution.py:387
  220.8 1.2 copy.15
  (1 shorter events, 0.0 us)
Async XLA Ops:
  2.2 1.9 copy-start.6
  2.2 1.9 copy-start.7
  2.2 1.9 copy-start.8
  3.7 2.0 copy-start
  3.7 65.3 %slice-start = ((s8[6291456]{0:T(1024)(128)(4,1)}), s8[4194304]{0:T(1024)(128)(4,1)S(1)}, s32[]{:S(2)}) async-start(s8[6291456]{0:T(1024)(128)(4,1)} %bitcast.11), calls=%async_computation | async-start | bytes 8388608
  5.7 2.3 %copy-start.1 = (bf16[3,768,768]{2,1,0:T(8,128)(2,1)S(1)}, bf16[3,768,768]{2,1,0:T(8,128)(2,1)}, u32[]{:S(2)}) copy-start(bf16[3,768,768]{2,1,0:T(8,128)(2,1)} %wn_ref.5) | copy-start | bytes 10616836
  7.9 61.0 %slice-start.1 = ((s8[6291456]{0:T(1024)(128)(4,1)}), s8[2097152]{0:T(1024)(128)(4,1)S(1)}, s32[]{:S(2)}) async-start(s8[6291456]{0:T(1024)(128)(4,1)} %bitcast.11), calls=%async_computation.1 | async-start | bytes 4194304
  65.9 3.1 %copy-start.4 = (bf16[10,3088,128]{2,1,0:T(8,128)(2,1)}, bf16[10,3088,128]{2,1,0:T(8,128)(2,1)S(1)}, u32[]{:S(2)}) copy-start(bf16[10,3088,128]{2,1,0:T(8,128)(2,1)S(1)} %get-tuple-element.15) | copy-start | bytes 23715844
  69.0 10.5 %copy-start.2 = (bf16[3,768,768]{2,1,0:T(8,128)(2,1)S(1)}, bf16[3,768,768]{2,1,0:T(8,128)(2,1)}, u32[]{:S(2)}) copy-start(bf16[3,768,768]{2,1,0:T(8,128)(2,1)} %wn_ref.5) | copy-start | bytes 10616836
  136.3 3.1 %copy-start.5 = (bf16[10,3088,128]{2,1,0:T(8,128)(2,1)}, bf16[10,3088,128]{2,1,0:T(8,128)(2,1)S(1)}, u32[]{:S(2)}) copy-start(bf16[10,3088,128]{2,1,0:T(8,128)(2,1)S(1)} %get-tuple-element.18) | copy-start | bytes 23715844
  206.8 3.1 %copy-start.3 = (bf16[10,3088,128]{2,1,0:T(8,128)(2,1)}, bf16[10,3088,128]{2,1,0:T(8,128)(2,1)S(1)}, u32[]{:S(2)}) copy-start(bf16[10,3088,128]{2,1,0:T(8,128)(2,1)S(1)} %get-tuple-element.21) | copy-start | bytes 23715844

commit v4 on v3

--- a/solution.py
+++ b/solution.py
@@ -16,11 +16,12 @@
 PACK = 192
 HEAD = 16
 CHUNKS = (4, 4, 4, 4)
-AHEAD = 1
+GROUPS = 4
+AHEAD = 2
 PLACES = 9
 UNROLL = 8
-EXCHANGE_BYTES = 32 * 1024 * 1024
-AGGREGATE_BYTES = 40 * 1024 * 1024
+EXCHANGE_BYTES = 14 * 1024 * 1024
+AGGREGATE_BYTES = 17 * 1024 * 1024
 
 
 def offset(d):
@@ -34,7 +35,7 @@
     return first, rest
 
 
-def order_tiles(count, dst, src, g_ref, idx_ref):
+def order_tiles(count, dst, src, core, g_ref, idx_ref):
     f32 = jnp.float32
     wide = 2 * LANES
     slot_rows = g_ref.shape[1]
@@ -66,7 +67,10 @@
     for d in range(PEERS):
         spot = 4 - offset(d)
         table = g_ref[spot, :HEAD, :].astype(f32)[d:d + 1]
-        first = jnp.where(short.astype(f32) < table[:, SLOTS:SLOTS + 1], float(spot * slot_rows + HEAD) + PACK * table,
+        block = table
+        if spot in (0, 8):
+            block = jnp.where(core == spot // 8, short.astype(f32), table)
+        first = jnp.where(short.astype(f32) < table[:, SLOTS:SLOTS + 1], float(spot * slot_rows + HEAD) + PACK * block,
                           float(zero_row))
         first = jnp.where(short < SLOTS, first, 0.0)
         offs = offs + pltpu.roll(jnp.broadcast_to(first, (8, LANES)), 16 + SLOTS * d, 1)[:1]
@@ -86,7 +90,7 @@
 
 
 def exchange(layer, count_ref, h_ref, tab_ref, ws_ref, wn_ref, b_ref, dst_ref, src_ref, g_ref, s_ref, idx_ref,
-             held, lhs, raw, w_ref, load_sem, tab_sem, raw_sem, ysend, yrecv, xsend, xrecv, psend, precv):
+             held, lhs, raw, w_ref, picked, load_sem, tab_sem, raw_sem, ysend, yrecv, xsend, xrecv, psend, precv):
     i = lax.axis_index("dom")
     y = lax.axis_index("feat")
     n_dom = lax.axis_size("dom")
@@ -185,7 +189,15 @@
                 low, top, pltpu.roll(bot, 64, 1)).astype(jnp.bfloat16)
             s_ref[base + BLK:base + PACK, :] = jnp.where(low, pltpu.roll(top, 64, 1), bot)
 
-    ours, first, second = [], [], []
+    whole_to = x_down + core * (x_up - x_down)
+    whole_from, whole_at = 6 - 4 * core, 8 - 8 * core
+    list_to = x_up + core * (x_down - x_up)
+    list_from, list_at = 2 + 4 * core, 8 * core
+    ours, first, second, listed = [], [], [], []
+
+    def group(m):
+        size = sum(CHUNKS) // GROUPS * PACK
+        return pl.ds(0, HEAD + size) if m == 0 else pl.ds(HEAD + m * size, size)
 
     def send_own(n):
         src = g_ref.at[4, grows(n)]
@@ -197,27 +209,45 @@
         ours.append((a, b, c))
         sent.extend([a, b, c])
 
-    def relay_one(n):
-        a, b, _ = ours[n]
-        a.wait_recv()
-        u = remote(g_ref.at[2, grows(n)], g_ref.at[0, grows(n)], xsend.at[2, n], xrecv.at[2, n], x_up, y)
-        pu = remote(g_ref.at[2, grows(n)], g_ref.at[1 + 2 * core, grows(n)], psend.at[1, n], precv.at[1, n], partner, y)
-        u.start()
-        pu.start()
-        b.wait_recv()
-        v = remote(g_ref.at[6, grows(n)], g_ref.at[8, grows(n)], xsend.at[3, n], xrecv.at[3, n], x_down, y)
-        pv = remote(g_ref.at[6, grows(n)], g_ref.at[5 + 2 * core, grows(n)], psend.at[2, n], precv.at[2, n], partner, y)
-        v.start()
-        pv.start()
-        first.append((u, v, pu, pv))
-        sent.extend([u, v, pu, pv])
-
-    def relay_two(n):
-        u, v, _, _ = first[n]
-        u.wait_recv()
-        v.wait_recv()
-        c = remote(g_ref.at[8 - 8 * core, grows(n)], g_ref.at[7 - 6 * core, grows(n)], psend.at[3, n], precv.at[3, n],
-                   partner, y)
+    def relay_group(m):
+        per = NC // GROUPS
+        for n in range(m * per, (m + 1) * per):
+            ours[n][0].wait_recv()
+            ours[n][1].wait_recv()
+        u = remote(g_ref.at[whole_from, group(m)], g_ref.at[whole_at, group(m)], xsend.at[2, m], xrecv.at[2, m], whole_to, y)
+        pu = remote(g_ref.at[2, group(m)], g_ref.at[1 + 2 * core, group(m)], psend.at[1, m], precv.at[1, m], partner, y)
+        pv = remote(g_ref.at[6, group(m)], g_ref.at[5 + 2 * core, group(m)], psend.at[2, m], precv.at[2, m], partner, y)
+        for copy in (u, pu, pv):
+            copy.start()
+        first.append((u, pu, pv))
+        sent.extend([u, pu, pv])
+
+    def relay_list():
+        picked[:HEAD, :] = g_ref[list_from, :HEAD, :]
+        table = g_ref[list_from, :HEAD, :].astype(jnp.float32)
+        wanted = jnp.where(core == 1, table[7:8], table[6:7])
+        short = lax.broadcasted_iota(jnp.int32, (1, LANES), 1)
+
+        def pick(s, carry):
+            block = jnp.sum(jnp.where(short == s, wanted, 0.0), axis=1, keepdims=True)
+            block = jnp.broadcast_to(block, (16, LANES))
+            total = jnp.zeros((PACK // 16, 16, LANES), jnp.bfloat16)
+            for j in range(sum(CHUNKS)):
+                one = jnp.where(block == float(j), 1.0, 0.0).astype(jnp.bfloat16)
+                rows = g_ref[list_from, HEAD + j * PACK:HEAD + (j + 1) * PACK, :]
+                total = total + rows.reshape(PACK // 16, 16, LANES) * one[None]
+            picked[pl.ds(pl.multiple_of(HEAD + s * PACK, 16), PACK), :] = total.reshape(PACK, LANES)
+            return carry
+
+        lax.fori_loop(0, SLOTS, pick, 0)
+        copy = remote(picked, g_ref.at[list_at, pl.ds(0, HEAD + SLOTS * PACK)], xsend.at[3, 0], xrecv.at[3, 0], list_to, y)
+        copy.start()
+        listed.append(copy)
+        sent.append(copy)
+
+    def relay_two(m):
+        first[m][0].wait_recv()
+        c = remote(g_ref.at[whole_at, group(m)], g_ref.at[7 - 6 * core, group(m)], psend.at[3, m], precv.at[3, m], partner, y)
         c.start()
         second.append(c)
         sent.append(c)
@@ -238,30 +268,31 @@
     bias = jnp.concatenate([jnp.zeros((1, LANES), jnp.float32), b_first, jnp.zeros((1, 64), jnp.float32), b_rest], axis=1)
 
     tab_load.wait()
+    relays = [gather_relay(0)]
     for n in range(NC):
-        a, b = gather_relay(n)
-        a.wait_recv()
-        b.wait_recv()
+        for relay in relays[n]:
+            relay.wait_recv()
         project(n)
         send_own(n)
-        if n >= 1:
-            relay_one(n - 1)
-        if n >= 2:
-            relay_two(n - 2)
-    relay_one(NC - 1)
-    for n in range(1):
+        if n + 1 < NC:
+            relays.append(gather_relay(n + 1))
+        for m in range(GROUPS):
+            if n == min((m + 1) * (NC // GROUPS), NC - 1):
+                relay_group(m)
+    relay_list()
+    for m in range(GROUPS):
+        relay_two(m)
+    for n in range(NC):
         ours[n][2].wait_recv()
-        first[n][2].wait_recv()
-        first[n][3].wait_recv()
-        second[n].wait_recv()
-    order_tiles(count_ref[0], dst_ref[...], src_ref[...], g_ref, idx_ref)
-    for n in range(max(NC - 2, 0), NC):
-        relay_two(n)
-    for n in range(1, NC):
-        ours[n][2].wait_recv()
-        first[n][2].wait_recv()
-        first[n][3].wait_recv()
-        second[n].wait_recv()
+    for m in range(GROUPS):
+        first[m][1].wait_recv()
+        first[m][2].wait_recv()
+        second[m].wait_recv()
+    listed[0].wait_recv()
+    if layer == 0:
+        order_tiles(count_ref[0], dst_ref[...], src_ref[...], core, g_ref, idx_ref)
+    else:
+        idx_ref[...] = jnp.zeros(idx_ref.shape, idx_ref.dtype)
     for copy in sent:
         copy.wait_send()
 
@@ -337,7 +368,8 @@
 
     NC = len(CHUNKS)
     vmem = pl.BlockSpec(memory_space=pltpu.VMEM)
-    hbm = pl.BlockSpec(memory_space=pl.ANY)
+    anywhere = pl.BlockSpec(memory_space=pl.ANY)
+    hbm = pl.BlockSpec(memory_space=pltpu.HBM)
 
     def exchange_call(layer):
         return pl.pallas_call(
@@ -347,13 +379,14 @@
                 jax.ShapeDtypeStruct((packed_rows, LANES), jnp.float32),
                 jax.ShapeDtypeStruct((8, 2 * LANES), jnp.int32),
             ),
-            in_specs=[pl.BlockSpec(memory_space=pltpu.SMEM), hbm, hbm, hbm, hbm, vmem, vmem, vmem],
+            in_specs=[pl.BlockSpec(memory_space=pltpu.SMEM), anywhere, anywhere, hbm, hbm, vmem, vmem, vmem],
             out_specs=(vmem, vmem, vmem),
             scratch_shapes=[
                 pltpu.VMEM((4, packed_rows, LANES), jnp.bfloat16),
                 pltpu.VMEM((max(CHUNKS) * BLK, 768), jnp.bfloat16),
                 pltpu.VMEM((2, 768, 2 * LANES), jnp.bfloat16),
                 pltpu.VMEM((768, 3 * LANES), jnp.bfloat16),
+                pltpu.VMEM((HEAD + SLOTS * PACK, LANES), jnp.bfloat16),
                 pltpu.SemaphoreType.DMA((NC,)),
                 pltpu.SemaphoreType.DMA,
                 pltpu.SemaphoreType.DMA((2,)),
@@ -382,7 +415,8 @@
 
     dsts, srcs = tile_dst[None, :], tile_src[None, :]
     for layer in range(LAYERS):
-        g, s, idx = exchange_call(layer)(tile_count, hidden, table, w_self, w_nbr, bias, dsts, srcs)
+        g, s, order = exchange_call(layer)(tile_count, hidden, table, w_self, w_nbr, bias, dsts, srcs)
+        idx = order if layer == 0 else idx
         g = g.reshape((PLACES + 1) * slot_rows, LANES)
         hidden = aggregate_call(layer == LAYERS - 1)(idx, g, tile_vals, s)
     return hidden

time: 224 us -> 201 us (0.90)
  Pallas kernels: 204 us -> 191 us
  local copies, waits for them, and re-layouts: 16 us -> 6.82 us
    pallas_call x3, Pallas kernels: 31.5 us -> 21.4 us  [per_device(): hidden = aggregate_call(layer == LAYERS - 1)(idx, g, tile_vals, s)]
    unnamed x22 -> x16, local copies, waits for them, and re-layouts: 13 us -> 3.83 us
where the time goes in v4:
time: 201 us
  Pallas kernels  191 us (95%)
  local copies, waits for them, and re-layouts  6.82 us (3%)
    pallas_call x3, Pallas kernels, per_device(): exchange_call(layer)  170 us
    pallas_call x3, Pallas kernels, per_device(): hidden = aggregate_call(layer == LAYERS - 1)(idx, g, tile_vals, s)  21.4 us

profile of v4, /device:TPU:0, one launch (start us, length us, event | category | flops | bytes accessed | tf_op | source)
XLA Modules:
  0.0 200.7 jit_solution(8027259217488258071)
XLA Ops:
  0.7 0.7 convert_bitcast_fusion.1
  1.3 0.1 copy.14
  1.4 0.7 convert_bitcast_fusion
  2.1 0.1 fusion.5.tab_ref
  2.2 0.0 copy-start.3
  2.2 0.0 copy-start.4
  2.2 0.0 copy-start.5
  2.2 1.5 copy.16
  3.7 0.0 copy-start
  3.7 0.0 slice-start
  3.7 0.1 slice.12
  3.8 0.1 fusion.6
  3.9 0.2 maximum_maximum_fusion
  4.1 0.0 copy-done.3
  4.1 0.0 copy-done.4
  4.1 0.0 copy-done.5
  4.1 1.5 copy-done
  5.7 0.0 copy-start.1
  5.7 2.3 %copy-done.1 = bf16[3,768,768]{2,1,0:T(8,128)(2,1)S(1)} copy-done((bf16[3,768,768]{2,1,0:T(8,128)(2,1)S(1)}, bf16[3,768,768]{2,1,0:T(8,128)(2,1)}, u32[]{:S(2)}) %copy-start.1) | copy-done | bytes 3538968
  7.9 0.0 slice-start.1
  7.9 59.9 %exchange0.1 = (bf16[10,3088,128]{2,1,0:T(8,128)(2,1)S(1)}, f32[3072,128]{1,0:T(8,128)S(1)}, s32[8,256]{1,0:T(8,128)S(1)}) custom-call(s32[1]{0:T(128)S(6)} %copy.17.count_ref, bf16[3072,128]{1,0:T(8,128)(2,1)S(1)} %bitcast.16, bf16[16,128]{1,0:T(8,128)(2,1)S(1)} %fusion.5.tab_ref, bf16[3,768,768]{2,1,0:T(8,128)(2,1)S(1)} %copy-done, ...), custom_call_target="tpu_custom_call" | custom-call | tf_op jit(solution)/shard_map/exchange0/pallas_call | solution.py:418
  67.9 0.0 slice-done
  67.9 0.0 slice-done.1
  67.9 0.0 copy-start.2
  67.9 6.9 %aggregate.2.h_ref = bf16[3072,128]{1,0:T(8,128)(2,1)S(1)} custom-call(s32[8,256]{1,0:T(8,128)S(1)} %get-tuple-element.12.idx, bf16[30880,128]{1,0:T(8,128)(2,1)S(1)} %bitcast.14, bf16[192,128,128]{2,1,0:T(8,128)(2,1)S(1)} %bitcast.12, f32[3072,128]{1,0:T(8,128)S(1)} %get-tuple-element.14.s_ref), custom_call_target="tpu_custom_call" | custom-call | tf_op jit(solution)/shard_map/aggregate/pallas_call | solution.py:421
  74.8 0.0 copy-done.2
  74.8 55.1 %exchange1.1 = (bf16[10,3088,128]{2,1,0:T(8,128)(2,1)S(1)}, f32[3072,128]{1,0:T(8,128)S(1)}, s32[8,256]{1,0:T(8,128)}) custom-call(s32[1]{0:T(128)S(6)} %copy.17.count_ref, bf16[3072,128]{1,0:T(8,128)(2,1)S(1)} %aggregate.2.h_ref, bf16[16,128]{1,0:T(8,128)(2,1)S(1)} %fusion.5.tab_ref, bf16[3,768,768]{2,1,0:T(8,128)(2,1)S(1)} %copy-done, ...), custom_call_target="tpu_custom_call" | custom-call | tf_op jit(solution)/shard_map/exchange1/pallas_call | solution.py:418
  129.9 6.9 %aggregate.3.h_ref = bf16[3072,128]{1,0:T(8,128)(2,1)S(1)} custom-call(s32[8,256]{1,0:T(8,128)S(1)} %get-tuple-element.12.idx, bf16[30880,128]{1,0:T(8,128)(2,1)S(1)} %bitcast.15, bf16[192,128,128]{2,1,0:T(8,128)(2,1)S(1)} %bitcast.12, f32[3072,128]{1,0:T(8,128)S(1)} %get-tuple-element.16.s_ref), custom_call_target="tpu_custom_call" | custom-call | tf_op jit(solution)/shard_map/aggregate/pallas_call | solution.py:421
  136.8 55.0 %exchange2.1 = (bf16[10,3088,128]{2,1,0:T(8,128)(2,1)S(1)}, f32[3072,128]{1,0:T(8,128)S(1)}, s32[8,256]{1,0:T(8,128)}) custom-call(s32[1]{0:T(128)S(6)} %copy.17.count_ref, bf16[3072,128]{1,0:T(8,128)(2,1)S(1)} %aggregate.3.h_ref, bf16[16,128]{1,0:T(8,128)(2,1)S(1)} %fusion.5.tab_ref, bf16[3,768,768]{2,1,0:T(8,128)(2,1)S(1)} %copy-done, ...), custom_call_target="tpu_custom_call" | custom-call | tf_op jit(solution)/shard_map/exchange2/pallas_call | solution.py:418
  191.8 7.6 %aggregate_last.1 = bf16[2048,192]{1,0:T(8,128)(2,1)S(1)} custom-call(s32[8,256]{1,0:T(8,128)S(1)} %get-tuple-element.12.idx, bf16[30880,128]{1,0:T(8,128)(2,1)S(1)} %bitcast.13, bf16[192,128,128]{2,1,0:T(8,128)(2,1)S(1)} %bitcast.12, f32[3072,128]{1,0:T(8,128)S(1)} %get-tuple-element.18.s_ref), custom_call_target="tpu_custom_call" | custom-call | tf_op jit(solution)/shard_map/aggregate_last/pallas_call | solution.py:421
  199.4 1.2 copy.15
  (1 shorter events, 0.0 us)
Async XLA Ops:
  2.2 1.9 copy-start.3
  2.2 1.9 copy-start.4
  2.2 1.9 copy-start.5
  3.7 2.0 copy-start
  3.7 64.2 %slice-start = ((s8[6291456]{0:T(1024)(128)(4,1)}), s8[4194304]{0:T(1024)(128)(4,1)S(1)}, s32[]{:S(2)}) async-start(s8[6291456]{0:T(1024)(128)(4,1)} %bitcast.11), calls=%async_computation | async-start | bytes 8388608
  5.7 2.3 %copy-start.1 = (bf16[3,768,768]{2,1,0:T(8,128)(2,1)S(1)}, bf16[3,768,768]{2,1,0:T(8,128)(2,1)}, u32[]{:S(2)}) copy-start(bf16[3,768,768]{2,1,0:T(8,128)(2,1)} %wn_ref.5) | copy-start | bytes 10616836
  7.9 60.0 %slice-start.1 = ((s8[6291456]{0:T(1024)(128)(4,1)}), s8[2097152]{0:T(1024)(128)(4,1)S(1)}, s32[]{:S(2)}) async-start(s8[6291456]{0:T(1024)(128)(4,1)} %bitcast.11), calls=%async_computation.1 | async-start | bytes 4194304
  67.9 6.9 %copy-start.2 = (bf16[3,768,768]{2,1,0:T(8,128)(2,1)S(1)}, bf16[3,768,768]{2,1,0:T(8,128)(2,1)}, u32[]{:S(2)}) copy-start(bf16[3,768,768]{2,1,0:T(8,128)(2,1)} %wn_ref.5) | copy-start | bytes 10616836

commit v5 on v4

--- a/solution.py
+++ b/solution.py
@@ -19,7 +19,7 @@
 GROUPS = 4
 AHEAD = 2
 PLACES = 9
-UNROLL = 8
+UNROLL = 26
 EXCHANGE_BYTES = 14 * 1024 * 1024
 AGGREGATE_BYTES = 17 * 1024 * 1024
 
@@ -89,8 +89,8 @@
         idx_ref[k:k + 1, :] = row.astype(jnp.int32)
 
 
-def exchange(layer, count_ref, h_ref, tab_ref, ws_ref, wn_ref, b_ref, dst_ref, src_ref, g_ref, s_ref, idx_ref,
-             held, lhs, raw, w_ref, picked, load_sem, tab_sem, raw_sem, ysend, yrecv, xsend, xrecv, psend, precv):
+def exchange(layer, count_ref, h_ref, list_ref, many_ref, ws_ref, wn_ref, b_ref, dst_ref, src_ref, g_ref, s_ref, idx_ref,
+             held, lhs, raw, w_ref, picked, tab, load_sem, raw_sem, ysend, yrecv, xsend, xrecv, psend, precv):
     i = lax.axis_index("dom")
     y = lax.axis_index("feat")
     n_dom = lax.axis_size("dom")
@@ -119,8 +119,6 @@
     loads = [pltpu.make_async_copy(h_ref.at[hrows(n)], held.at[y, hrows(n)], load_sem.at[n]) for n in range(NC)]
     for load in loads:
         load.start()
-    tab_load = pltpu.make_async_copy(tab_ref, g_ref.at[4, pl.ds(0, HEAD)], tab_sem)
-    tab_load.start()
     window = pl.ds(pl.multiple_of((3 * y // 2) * LANES, LANES), 2 * LANES)
     raws = [pltpu.make_async_copy(ref.at[layer, :, window], raw.at[k], raw_sem.at[k]) for k, ref in enumerate((wn_ref, ws_ref))]
     for load in raws:
@@ -267,7 +265,13 @@
     b_first, b_rest = cut(b_ref[layer:layer + 1, window], odd)
     bias = jnp.concatenate([jnp.zeros((1, LANES), jnp.float32), b_first, jnp.zeros((1, 64), jnp.float32), b_rest], axis=1)
 
-    tab_load.wait()
+    tab[...] = jnp.zeros(tab.shape, jnp.float32)
+    tab[:PEERS, :SLOTS] = list_ref[...].astype(jnp.float32)
+    diagonal = lax.broadcasted_iota(jnp.int32, (PEERS, PEERS), 0) == lax.broadcasted_iota(jnp.int32, (PEERS, PEERS), 1)
+    many = jnp.where(diagonal, many_ref[...].astype(jnp.float32), 0.0)
+    tab[:PEERS, SLOTS:SLOTS + 1] = jnp.sum(many, axis=1, keepdims=True)
+    g_ref[4, :HEAD, :] = tab[...].astype(jnp.bfloat16)
+
     relays = [gather_relay(0)]
     for n in range(NC):
         for relay in relays[n]:
@@ -363,9 +367,6 @@
         [f3[..., :128], jnp.concatenate([f3[:, :64, 128:], f3[:, 64:, 128:]], axis=2)], axis=1
     ).reshape(packed_rows, LANES)
 
-    table = jnp.concatenate([send_blocks[0], send_count[0][:, None]], axis=1).astype(jnp.bfloat16)
-    table = jnp.pad(table, ((0, HEAD - PEERS), (0, LANES - SLOTS - 1)))
-
     NC = len(CHUNKS)
     vmem = pl.BlockSpec(memory_space=pltpu.VMEM)
     anywhere = pl.BlockSpec(memory_space=pl.ANY)
@@ -379,7 +380,7 @@
                 jax.ShapeDtypeStruct((packed_rows, LANES), jnp.float32),
                 jax.ShapeDtypeStruct((8, 2 * LANES), jnp.int32),
             ),
-            in_specs=[pl.BlockSpec(memory_space=pltpu.SMEM), anywhere, anywhere, hbm, hbm, vmem, vmem, vmem],
+            in_specs=[pl.BlockSpec(memory_space=pltpu.SMEM), anywhere, vmem, vmem, hbm, hbm, vmem, vmem, vmem],
             out_specs=(vmem, vmem, vmem),
             scratch_shapes=[
                 pltpu.VMEM((4, packed_rows, LANES), jnp.bfloat16),
@@ -387,8 +388,8 @@
                 pltpu.VMEM((2, 768, 2 * LANES), jnp.bfloat16),
                 pltpu.VMEM((768, 3 * LANES), jnp.bfloat16),
                 pltpu.VMEM((HEAD + SLOTS * PACK, LANES), jnp.bfloat16),
+                pltpu.VMEM((HEAD, LANES), jnp.float32),
                 pltpu.SemaphoreType.DMA((NC,)),
-                pltpu.SemaphoreType.DMA,
                 pltpu.SemaphoreType.DMA((2,)),
             ] + [pltpu.SemaphoreType.DMA((4, NC)) for _ in range(6)],
             compiler_params=pltpu.CompilerParams(
@@ -414,8 +415,9 @@
         )
 
     dsts, srcs = tile_dst[None, :], tile_src[None, :]
+    ws, wn = (pltpu.with_memory_space_constraint(w, pltpu.HBM) for w in (w_self, w_nbr))
     for layer in range(LAYERS):
-        g, s, order = exchange_call(layer)(tile_count, hidden, table, w_self, w_nbr, bias, dsts, srcs)
+        g, s, order = exchange_call(layer)(tile_count, hidden, send_blocks[0], send_count, ws, wn, bias, dsts, srcs)
         idx = order if layer == 0 else idx
         g = g.reshape((PLACES + 1) * slot_rows, LANES)
         hidden = aggregate_call(layer == LAYERS - 1)(idx, g, tile_vals, s)

time: 201 us -> 191 us (0.950)
  Pallas kernels: 191 us -> 187 us
  local copies, waits for them, and re-layouts: 6.82 us -> 3.14 us
    pallas_call x3, Pallas kernels: 21.4 us -> 16.6 us  [per_device(): hidden = aggregate_call(layer == LAYERS - 1)(idx, g, tile_vals, s)]
    unnamed x16 -> x14, local copies, waits for them, and re-layouts: 3.83 us -> 0.28 us
where the time goes in v5:
time: 191 us
  Pallas kernels  187 us (98%)
  local copies, waits for them, and re-layouts  3.14 us (2%)
    pallas_call x3, Pallas kernels, per_device(): exchange_call(layer)  170 us
    pallas_call x3, Pallas kernels, per_device(): hidden = aggregate_call(layer == LAYERS - 1)(idx, g, tile_vals, s)  16.6 us

profile of v5, /device:TPU:0, one launch (start us, length us, event | category | flops | bytes accessed | tf_op | source)
XLA Modules:
  0.0 190.7 jit_solution(12856044461543846150)
XLA Ops:
  0.7 1.4 copy.15
  2.1 0.0 copy-start
  2.1 0.0 copy-start.1
  2.1 0.0 copy-start.2
  2.1 0.0 copy-start.3
  2.1 0.0 copy-start.4
  2.2 0.0 slice-start
  2.2 0.1 slice.12
  2.3 0.1 fusion
  2.4 0.2 maximum_maximum_fusion
  2.6 0.2 copy-done
  2.8 0.0 copy-done.1
  2.8 0.0 copy-done.2
  2.8 0.0 copy-done.3
  2.8 0.0 copy-done.4
  2.8 0.0 slice-start.1
  2.8 60.0 %exchange0.1 = (bf16[10,3088,128]{2,1,0:T(8,128)(2,1)S(1)}, f32[3072,128]{1,0:T(8,128)S(1)}, s32[8,256]{1,0:T(8,128)S(1)}) custom-call(s32[1]{0:T(128)S(6)} %copy.16.count_ref, bf16[3072,128]{1,0:T(8,128)(2,1)S(1)} %bitcast.13, s32[8,8]{1,0:T(8,128)S(1)} %bitcast.14, s32[1,8]{1,0:T(1,128)S(1)} %copy-done.4, bf16[3,768,768]{2,1,0:T(8,128)(2,1)} %ws_ref.5, ...), custom_call_target="tpu_custom_call" | custom-call | tf_op jit(solution)/shard_map/exchange0/pallas_call | solution.py:420
  62.8 0.0 slice-done
  62.8 0.0 slice-done.1
  62.9 5.3 %aggregate.2.h_ref = bf16[3072,128]{1,0:T(8,128)(2,1)S(1)} custom-call(s32[8,256]{1,0:T(8,128)S(1)} %get-tuple-element.12.idx, bf16[30880,128]{1,0:T(8,128)(2,1)S(1)} %bitcast.11, bf16[192,128,128]{2,1,0:T(8,128)(2,1)S(1)} %bitcast.9, f32[3072,128]{1,0:T(8,128)S(1)} %get-tuple-element.14.s_ref), custom_call_target="tpu_custom_call" | custom-call | tf_op jit(solution)/shard_map/aggregate/pallas_call | solution.py:423
  68.1 55.0 %exchange1.1 = (bf16[10,3088,128]{2,1,0:T(8,128)(2,1)S(1)}, f32[3072,128]{1,0:T(8,128)S(1)}, s32[8,256]{1,0:T(8,128)}) custom-call(s32[1]{0:T(128)S(6)} %copy.16.count_ref, bf16[3072,128]{1,0:T(8,128)(2,1)S(1)} %aggregate.2.h_ref, s32[8,8]{1,0:T(8,128)S(1)} %bitcast.15, s32[1,8]{1,0:T(1,128)S(1)} %copy-done.4, bf16[3,768,768]{2,1,0:T(8,128)(2,1)} %ws_ref.5, ...), custom_call_target="tpu_custom_call" | custom-call | tf_op jit(solution)/shard_map/exchange1/pallas_call | solution.py:420
  123.2 5.3 %aggregate.3.h_ref = bf16[3072,128]{1,0:T(8,128)(2,1)S(1)} custom-call(s32[8,256]{1,0:T(8,128)S(1)} %get-tuple-element.12.idx, bf16[30880,128]{1,0:T(8,128)(2,1)S(1)} %bitcast.12, bf16[192,128,128]{2,1,0:T(8,128)(2,1)S(1)} %bitcast.9, f32[3072,128]{1,0:T(8,128)S(1)} %get-tuple-element.16.s_ref), custom_call_target="tpu_custom_call" | custom-call | tf_op jit(solution)/shard_map/aggregate/pallas_call | solution.py:423
  128.4 54.9 %exchange2.1 = (bf16[10,3088,128]{2,1,0:T(8,128)(2,1)S(1)}, f32[3072,128]{1,0:T(8,128)S(1)}, s32[8,256]{1,0:T(8,128)}) custom-call(s32[1]{0:T(128)S(6)} %copy.16.count_ref, bf16[3072,128]{1,0:T(8,128)(2,1)S(1)} %aggregate.3.h_ref, s32[8,8]{1,0:T(8,128)S(1)} %bitcast.16, s32[1,8]{1,0:T(1,128)S(1)} %copy-done.4, bf16[3,768,768]{2,1,0:T(8,128)(2,1)} %ws_ref.5, ...), custom_call_target="tpu_custom_call" | custom-call | tf_op jit(solution)/shard_map/exchange2/pallas_call | solution.py:420
  183.4 6.1 %aggregate_last.1 = bf16[2048,192]{1,0:T(8,128)(2,1)S(1)} custom-call(s32[8,256]{1,0:T(8,128)S(1)} %get-tuple-element.12.idx, bf16[30880,128]{1,0:T(8,128)(2,1)S(1)} %bitcast.10, bf16[192,128,128]{2,1,0:T(8,128)(2,1)S(1)} %bitcast.9, f32[3072,128]{1,0:T(8,128)S(1)} %get-tuple-element.18.s_ref), custom_call_target="tpu_custom_call" | custom-call | tf_op jit(solution)/shard_map/aggregate_last/pallas_call | solution.py:423
  189.4 1.2 copy.14
  (1 shorter events, 0.0 us)
Async XLA Ops:
  2.1 0.7 copy-start
  2.1 0.7 copy-start.1
  2.1 0.7 copy-start.2
  2.1 0.7 copy-start.3
  2.1 0.7 copy-start.4
  2.2 60.7 %slice-start = ((s8[6291456]{0:T(1024)(128)(4,1)}), s8[4194304]{0:T(1024)(128)(4,1)S(1)}, s32[]{:S(2)}) async-start(s8[6291456]{0:T(1024)(128)(4,1)} %bitcast.8), calls=%async_computation | async-start | bytes 8388608
  2.8 60.0 %slice-start.1 = ((s8[6291456]{0:T(1024)(128)(4,1)}), s8[2097152]{0:T(1024)(128)(4,1)S(1)}, s32[]{:S(2)}) async-start(s8[6291456]{0:T(1024)(128)(4,1)} %bitcast.8), calls=%async_computation.1 | async-start | bytes 4194304

commit v6 on v5

--- a/solution.py
+++ b/solution.py
@@ -215,13 +215,14 @@
         u = remote(g_ref.at[whole_from, group(m)], g_ref.at[whole_at, group(m)], xsend.at[2, m], xrecv.at[2, m], whole_to, y)
         pu = remote(g_ref.at[2, group(m)], g_ref.at[1 + 2 * core, group(m)], psend.at[1, m], precv.at[1, m], partner, y)
         pv = remote(g_ref.at[6, group(m)], g_ref.at[5 + 2 * core, group(m)], psend.at[2, m], precv.at[2, m], partner, y)
-        for copy in (u, pu, pv):
-            copy.start()
+        u.start()
+        if m < GROUPS - 1:
+            pu.start()
+            pv.start()
         first.append((u, pu, pv))
         sent.extend([u, pu, pv])
 
-    def relay_list():
-        picked[:HEAD, :] = g_ref[list_from, :HEAD, :]
+    def pick_blocks(low_block, high_block):
         table = g_ref[list_from, :HEAD, :].astype(jnp.float32)
         wanted = jnp.where(core == 1, table[7:8], table[6:7])
         short = lax.broadcasted_iota(jnp.int32, (1, LANES), 1)
@@ -229,15 +230,23 @@
         def pick(s, carry):
             block = jnp.sum(jnp.where(short == s, wanted, 0.0), axis=1, keepdims=True)
             block = jnp.broadcast_to(block, (16, LANES))
-            total = jnp.zeros((PACK // 16, 16, LANES), jnp.bfloat16)
-            for j in range(sum(CHUNKS)):
+            place = pl.ds(pl.multiple_of(HEAD + s * PACK, 16), PACK)
+            if low_block == 0:
+                total = jnp.zeros((PACK // 16, 16, LANES), jnp.bfloat16)
+            else:
+                total = picked[place, :].reshape(PACK // 16, 16, LANES)
+            for j in range(low_block, high_block):
                 one = jnp.where(block == float(j), 1.0, 0.0).astype(jnp.bfloat16)
                 rows = g_ref[list_from, HEAD + j * PACK:HEAD + (j + 1) * PACK, :]
                 total = total + rows.reshape(PACK // 16, 16, LANES) * one[None]
-            picked[pl.ds(pl.multiple_of(HEAD + s * PACK, 16), PACK), :] = total.reshape(PACK, LANES)
+            picked[place, :] = total.reshape(PACK, LANES)
             return carry
 
         lax.fori_loop(0, SLOTS, pick, 0)
+
+    def relay_list():
+        picked[:HEAD, :] = g_ref[list_from, :HEAD, :]
+        pick_blocks(sum(CHUNKS[:-1]), sum(CHUNKS))
         copy = remote(picked, g_ref.at[list_at, pl.ds(0, HEAD + SLOTS * PACK)], xsend.at[3, 0], xrecv.at[3, 0], list_to, y)
         copy.start()
         listed.append(copy)
@@ -283,7 +292,11 @@
         for m in range(GROUPS):
             if n == min((m + 1) * (NC // GROUPS), NC - 1):
                 relay_group(m)
+                if m == GROUPS - 2:
+                    pick_blocks(0, sum(CHUNKS[:-1]))
     relay_list()
+    first[-1][1].start()
+    first[-1][2].start()
     for m in range(GROUPS):
         relay_two(m)
     for n in range(NC):

time: 191 us -> 189 us (0.990)
  Pallas kernels: 187 us -> 185 us
where the time goes in v6:
time: 189 us
  Pallas kernels  185 us (98%)
  local copies, waits for them, and re-layouts  3.14 us (2%)
    pallas_call x3, Pallas kernels, per_device(): exchange_call(layer)  168 us
    pallas_call x3, Pallas kernels, per_device(): hidden = aggregate_call(layer == LAYERS - 1)(idx, g, tile_vals, s)  16.6 us

profile of v6, /device:TPU:0, one launch (start us, length us, event | category | flops | bytes accessed | tf_op | source)
XLA Modules:
  0.0 189.0 jit_solution(10016174189993618044)
XLA Ops:
  0.7 1.4 copy.15
  2.1 0.0 copy-start
  2.1 0.0 copy-start.1
  2.1 0.0 copy-start.2
  2.1 0.0 copy-start.3
  2.1 0.0 copy-start.4
  2.2 0.0 slice-start
  2.2 0.1 slice.12
  2.3 0.1 fusion
  2.4 0.2 maximum_maximum_fusion
  2.6 0.2 copy-done
  2.8 0.0 copy-done.1
  2.8 0.0 copy-done.2
  2.8 0.0 copy-done.3
  2.8 0.0 copy-done.4
  2.8 0.0 slice-start.1
  2.8 59.3 %exchange0.1 = (bf16[10,3088,128]{2,1,0:T(8,128)(2,1)S(1)}, f32[3072,128]{1,0:T(8,128)S(1)}, s32[8,256]{1,0:T(8,128)S(1)}) custom-call(s32[1]{0:T(128)S(6)} %copy.16.count_ref, bf16[3072,128]{1,0:T(8,128)(2,1)S(1)} %bitcast.13, s32[8,8]{1,0:T(8,128)S(1)} %bitcast.14, s32[1,8]{1,0:T(1,128)S(1)} %copy-done.4, bf16[3,768,768]{2,1,0:T(8,128)(2,1)} %ws_ref.5, ...), custom_call_target="tpu_custom_call" | custom-call | tf_op jit(solution)/shard_map/exchange0/pallas_call | solution.py:433
  62.2 0.0 slice-done
  62.2 0.0 slice-done.1
  62.2 5.3 %aggregate.2.h_ref = bf16[3072,128]{1,0:T(8,128)(2,1)S(1)} custom-call(s32[8,256]{1,0:T(8,128)S(1)} %get-tuple-element.12.idx, bf16[30880,128]{1,0:T(8,128)(2,1)S(1)} %bitcast.11, bf16[192,128,128]{2,1,0:T(8,128)(2,1)S(1)} %bitcast.9, f32[3072,128]{1,0:T(8,128)S(1)} %get-tuple-element.14.s_ref), custom_call_target="tpu_custom_call" | custom-call | tf_op jit(solution)/shard_map/aggregate/pallas_call | solution.py:436
  67.5 53.4 %exchange1.1 = (bf16[10,3088,128]{2,1,0:T(8,128)(2,1)S(1)}, f32[3072,128]{1,0:T(8,128)S(1)}, s32[8,256]{1,0:T(8,128)}) custom-call(s32[1]{0:T(128)S(6)} %copy.16.count_ref, bf16[3072,128]{1,0:T(8,128)(2,1)S(1)} %aggregate.2.h_ref, s32[8,8]{1,0:T(8,128)S(1)} %bitcast.15, s32[1,8]{1,0:T(1,128)S(1)} %copy-done.4, bf16[3,768,768]{2,1,0:T(8,128)(2,1)} %ws_ref.5, ...), custom_call_target="tpu_custom_call" | custom-call | tf_op jit(solution)/shard_map/exchange1/pallas_call | solution.py:433
  120.9 5.3 %aggregate.3.h_ref = bf16[3072,128]{1,0:T(8,128)(2,1)S(1)} custom-call(s32[8,256]{1,0:T(8,128)S(1)} %get-tuple-element.12.idx, bf16[30880,128]{1,0:T(8,128)(2,1)S(1)} %bitcast.12, bf16[192,128,128]{2,1,0:T(8,128)(2,1)S(1)} %bitcast.9, f32[3072,128]{1,0:T(8,128)S(1)} %get-tuple-element.16.s_ref), custom_call_target="tpu_custom_call" | custom-call | tf_op jit(solution)/shard_map/aggregate/pallas_call | solution.py:436
  126.1 55.6 %exchange2.1 = (bf16[10,3088,128]{2,1,0:T(8,128)(2,1)S(1)}, f32[3072,128]{1,0:T(8,128)S(1)}, s32[8,256]{1,0:T(8,128)}) custom-call(s32[1]{0:T(128)S(6)} %copy.16.count_ref, bf16[3072,128]{1,0:T(8,128)(2,1)S(1)} %aggregate.3.h_ref, s32[8,8]{1,0:T(8,128)S(1)} %bitcast.16, s32[1,8]{1,0:T(1,128)S(1)} %copy-done.4, bf16[3,768,768]{2,1,0:T(8,128)(2,1)} %ws_ref.5, ...), custom_call_target="tpu_custom_call" | custom-call | tf_op jit(solution)/shard_map/exchange2/pallas_call | solution.py:433
  181.8 6.0 %aggregate_last.1 = bf16[2048,192]{1,0:T(8,128)(2,1)S(1)} custom-call(s32[8,256]{1,0:T(8,128)S(1)} %get-tuple-element.12.idx, bf16[30880,128]{1,0:T(8,128)(2,1)S(1)} %bitcast.10, bf16[192,128,128]{2,1,0:T(8,128)(2,1)S(1)} %bitcast.9, f32[3072,128]{1,0:T(8,128)S(1)} %get-tuple-element.18.s_ref), custom_call_target="tpu_custom_call" | custom-call | tf_op jit(solution)/shard_map/aggregate_last/pallas_call | solution.py:436
  187.8 1.2 copy.14
  (1 shorter events, 0.0 us)
Async XLA Ops:
  2.1 0.7 copy-start
  2.1 0.7 copy-start.1
  2.1 0.7 copy-start.2
  2.1 0.7 copy-start.3
  2.1 0.7 copy-start.4
  2.2 60.0 %slice-start = ((s8[6291456]{0:T(1024)(128)(4,1)}), s8[4194304]{0:T(1024)(128)(4,1)S(1)}, s32[]{:S(2)}) async-start(s8[6291456]{0:T(1024)(128)(4,1)} %bitcast.8), calls=%async_computation | async-start | bytes 8388608
  2.8 59.3 %slice-start.1 = ((s8[6291456]{0:T(1024)(128)(4,1)}), s8[2097152]{0:T(1024)(128)(4,1)S(1)}, s32[]{:S(2)}) async-start(s8[6291456]{0:T(1024)(128)(4,1)} %bitcast.8), calls=%async_computation.1 | async-start | bytes 4194304

commit v7 on v6

--- a/solution.py
+++ b/solution.py
@@ -19,9 +19,9 @@
 GROUPS = 4
 AHEAD = 2
 PLACES = 9
-UNROLL = 26
+UNROLL = 52
 EXCHANGE_BYTES = 14 * 1024 * 1024
-AGGREGATE_BYTES = 17 * 1024 * 1024
+AGGREGATE_BYTES = 22 * 1024 * 1024
 
 
 def offset(d):
@@ -202,8 +202,8 @@
         a = remote(src, g_ref.at[2, grows(n)], xsend.at[0, n], xrecv.at[0, n], x_up, y)
         b = remote(src, g_ref.at[6, grows(n)], xsend.at[1, n], xrecv.at[1, n], x_down, y)
         c = remote(src, g_ref.at[3 + 2 * core, grows(n)], psend.at[0, n], precv.at[0, n], partner, y)
-        for copy in (a, b, c):
-            copy.start()
+        a.start()
+        b.start()
         ours.append((a, b, c))
         sent.extend([a, b, c])
 
@@ -216,6 +216,7 @@
         pu = remote(g_ref.at[2, group(m)], g_ref.at[1 + 2 * core, group(m)], psend.at[1, m], precv.at[1, m], partner, y)
         pv = remote(g_ref.at[6, group(m)], g_ref.at[5 + 2 * core, group(m)], psend.at[2, m], precv.at[2, m], partner, y)
         u.start()
+        ours[m][2].start()
         if m < GROUPS - 1:
             pu.start()
             pv.start()

time: 189 us -> 188 us (level)
  no operation moved by 1% of the time
where the time goes in v7:
time: 188 us
  Pallas kernels  184 us (98%)
  local copies, waits for them, and re-layouts  3.14 us (2%)
    pallas_call x3, Pallas kernels, per_device(): exchange_call(layer)  168 us
    pallas_call x3, Pallas kernels, per_device(): hidden = aggregate_call(layer == LAYERS - 1)(idx, g, tile_vals, s)  15.9 us

profile of v7, /device:TPU:0, one launch (start us, length us, event | category | flops | bytes accessed | tf_op | source)
XLA Modules:
  0.0 188.5 jit_solution(15240271331630394945)
XLA Ops:
  0.7 1.4 copy.15
  2.1 0.0 copy-start
  2.1 0.0 copy-start.1
  2.1 0.0 copy-start.2
  2.1 0.0 copy-start.3
  2.1 0.0 copy-start.4
  2.2 0.0 slice-start
  2.2 0.1 slice.12
  2.3 0.1 fusion
  2.4 0.2 maximum_maximum_fusion
  2.6 0.2 copy-done
  2.8 0.0 copy-done.1
  2.8 0.0 copy-done.2
  2.8 0.0 copy-done.3
  2.8 0.0 copy-done.4
  2.8 0.0 slice-start.1
  2.8 59.3 %exchange0.1 = (bf16[10,3088,128]{2,1,0:T(8,128)(2,1)S(1)}, f32[3072,128]{1,0:T(8,128)S(1)}, s32[8,256]{1,0:T(8,128)S(1)}) custom-call(s32[1]{0:T(128)S(6)} %copy.16.count_ref, bf16[3072,128]{1,0:T(8,128)(2,1)S(1)} %bitcast.13, s32[8,8]{1,0:T(8,128)S(1)} %bitcast.14, s32[1,8]{1,0:T(1,128)S(1)} %copy-done.4, bf16[3,768,768]{2,1,0:T(8,128)(2,1)} %ws_ref.5, ...), custom_call_target="tpu_custom_call" | custom-call | tf_op jit(solution)/shard_map/exchange0/pallas_call | solution.py:434
  62.2 0.0 slice-done
  62.2 0.0 slice-done.1
  62.2 5.0 %aggregate.2.h_ref = bf16[3072,128]{1,0:T(8,128)(2,1)S(1)} custom-call(s32[8,256]{1,0:T(8,128)S(1)} %get-tuple-element.12.idx, bf16[30880,128]{1,0:T(8,128)(2,1)S(1)} %bitcast.11, bf16[192,128,128]{2,1,0:T(8,128)(2,1)S(1)} %bitcast.9, f32[3072,128]{1,0:T(8,128)S(1)} %get-tuple-element.14.s_ref), custom_call_target="tpu_custom_call" | custom-call | tf_op jit(solution)/shard_map/aggregate/pallas_call | solution.py:437
  67.2 53.3 %exchange1.1 = (bf16[10,3088,128]{2,1,0:T(8,128)(2,1)S(1)}, f32[3072,128]{1,0:T(8,128)S(1)}, s32[8,256]{1,0:T(8,128)}) custom-call(s32[1]{0:T(128)S(6)} %copy.16.count_ref, bf16[3072,128]{1,0:T(8,128)(2,1)S(1)} %aggregate.2.h_ref, s32[8,8]{1,0:T(8,128)S(1)} %bitcast.15, s32[1,8]{1,0:T(1,128)S(1)} %copy-done.4, bf16[3,768,768]{2,1,0:T(8,128)(2,1)} %ws_ref.5, ...), custom_call_target="tpu_custom_call" | custom-call | tf_op jit(solution)/shard_map/exchange1/pallas_call | solution.py:434
  120.6 5.2 %aggregate.3.h_ref = bf16[3072,128]{1,0:T(8,128)(2,1)S(1)} custom-call(s32[8,256]{1,0:T(8,128)S(1)} %get-tuple-element.12.idx, bf16[30880,128]{1,0:T(8,128)(2,1)S(1)} %bitcast.12, bf16[192,128,128]{2,1,0:T(8,128)(2,1)S(1)} %bitcast.9, f32[3072,128]{1,0:T(8,128)S(1)} %get-tuple-element.16.s_ref), custom_call_target="tpu_custom_call" | custom-call | tf_op jit(solution)/shard_map/aggregate/pallas_call | solution.py:437
  125.7 55.8 %exchange2.1 = (bf16[10,3088,128]{2,1,0:T(8,128)(2,1)S(1)}, f32[3072,128]{1,0:T(8,128)S(1)}, s32[8,256]{1,0:T(8,128)}) custom-call(s32[1]{0:T(128)S(6)} %copy.16.count_ref, bf16[3072,128]{1,0:T(8,128)(2,1)S(1)} %aggregate.3.h_ref, s32[8,8]{1,0:T(8,128)S(1)} %bitcast.16, s32[1,8]{1,0:T(1,128)S(1)} %copy-done.4, bf16[3,768,768]{2,1,0:T(8,128)(2,1)} %ws_ref.5, ...), custom_call_target="tpu_custom_call" | custom-call | tf_op jit(solution)/shard_map/exchange2/pallas_call | solution.py:434
  181.5 5.7 %aggregate_last.1 = bf16[2048,192]{1,0:T(8,128)(2,1)S(1)} custom-call(s32[8,256]{1,0:T(8,128)S(1)} %get-tuple-element.12.idx, bf16[30880,128]{1,0:T(8,128)(2,1)S(1)} %bitcast.10, bf16[192,128,128]{2,1,0:T(8,128)(2,1)S(1)} %bitcast.9, f32[3072,128]{1,0:T(8,128)S(1)} %get-tuple-element.18.s_ref), custom_call_target="tpu_custom_call" | custom-call | tf_op jit(solution)/shard_map/aggregate_last/pallas_call | solution.py:437
  187.2 1.2 copy.14
  (1 shorter events, 0.0 us)
Async XLA Ops:
  2.1 0.7 copy-start
  2.1 0.7 copy-start.1
  2.1 0.7 copy-start.2
  2.1 0.7 copy-start.3
  2.1 0.7 copy-start.4
  2.2 60.0 %slice-start = ((s8[6291456]{0:T(1024)(128)(4,1)}), s8[4194304]{0:T(1024)(128)(4,1)S(1)}, s32[]{:S(2)}) async-start(s8[6291456]{0:T(1024)(128)(4,1)} %bitcast.8), calls=%async_computation | async-start | bytes 8388608
  2.8 59.3 %slice-start.1 = ((s8[6291456]{0:T(1024)(128)(4,1)}), s8[2097152]{0:T(1024)(128)(4,1)S(1)}, s32[]{:S(2)}) async-start(s8[6291456]{0:T(1024)(128)(4,1)} %bitcast.8), calls=%async_computation.1 | async-start | bytes 4194304
